TPU v7x, 32 devices: a whole 2x2x4 slice. The times are simulated.
32 devices in a mesh: fsdp: 16 (over z, y, x), rep: 2 (over core).
Axes of the slice: x: 2, y: 2, z: 4, core: 2. Of those that a mesh axis runs over, the one named last changes fastest.
Arguments:
- tokens: bfloat16 [32, 512, 768], P(('fsdp', 'rep')), may hold values from -6 to 6
- boxes: int32 [32, 2, 512], P(('fsdp', 'rep')), may hold values from 0 to 999
- lengths: int32 [32], P(('fsdp', 'rep')), may hold values from 40 to 512, as said below
- cotangent: bfloat16 [32, 512, 768], P(('fsdp', 'rep')), may hold values from -6 to 6
- attn_weight: float32 [5, 768, 768], P(None, 'fsdp')
- up_weight: float32 [768, 3072], P('fsdp'), may hold values from -0.21875 to 0.21875
- down_weight: float32 [3072, 768], P('fsdp'), may hold values from -0.109375 to 0.109375
- vectors: float32 [12, 768], P(None, 'fsdp')
- attn_first: float32 [5, 768, 768], P(None, 'fsdp')
- up_first: float32 [768, 3072], P('fsdp')
- down_first: float32 [3072, 768], P('fsdp')
- vector_first: float32 [12, 768], P(None, 'fsdp')
- attn_second: float32 [5, 768, 768], P(None, 'fsdp')
- up_second: float32 [768, 3072], P('fsdp')
- down_second: float32 [3072, 768], P('fsdp')
- vector_second: float32 [12, 768], P(None, 'fsdp')
Outputs:
- layer_out: bfloat16 [32, 512, 768], P(('fsdp', 'rep'))
- token_grad: float32 [32, 512, 768], P(('fsdp', 'rep'))
- attn_new: float32 [5, 768, 768], P(None, 'fsdp')
- up_new: float32 [768, 3072], P('fsdp')
- down_new: float32 [3072, 768], P('fsdp')
- vectors_new: float32 [12, 768], P(None, 'fsdp')
- attn_first_new: float32 [5, 768, 768], P(None, 'fsdp')
- up_first_new: float32 [768, 3072], P('fsdp')
- down_first_new: float32 [3072, 768], P('fsdp')
- vector_first_new: float32 [12, 768], P(None, 'fsdp')
- attn_second_new: float32 [5, 768, 768], P(None, 'fsdp')
- up_second_new: float32 [768, 3072], P('fsdp')
- down_second_new: float32 [3072, 768], P('fsdp')
- vector_second_new: float32 [12, 768], P(None, 'fsdp')
- attn_copy: bfloat16 [5, 768, 768], P(None, 'fsdp')
- up_copy: bfloat16 [768, 3072], P('fsdp')
- down_copy: bfloat16 [3072, 768], P('fsdp')
- vector_copy: bfloat16 [12, 768], P(None, 'fsdp')
Inputs may be any that keep to these rules, and one draw needn't show every extreme that they name: `lengths`: some page has exactly 512 real tokens and another exactly 40.
All inputs are finite; a program needn't handle non-finite values.
Results may differ from a plain program's by a relative error of at most 0.014.
The roundings to bfloat16 on the way count: a program that leaves them out, or rounds other values in their place, can miss the bound.
Values may be sent and summed in bfloat16 or wider, within the bound.
No kernel may reach another device: no remote copies, remote signals or barrier semaphores. Data moves between devices by JAX's collectives and lax.ppermute only.
A program may use at most 192 MiB of HBM per device.

v0:
```python
from functools import partial
import math

import jax
import jax.numpy as jnp
from jax import lax
from jax.sharding import PartitionSpec as P

HEADS = 12
HEAD_DIM = 64
STEP = 7


EPS_NORM = 1e-12
EPS_ADAM = 1e-08
DECAY = 0.5
MASK_FILL = -1e30
WEIGHT_DECAY = 0.01
ATTN_RATES = (0.04, 0.04, 0.04, 0.2, 0.04)
UP_RATE = 0.04
DOWN_RATE = 0.02
VECTOR_RATE = 0.3


def contract(left_op, right_op, left_dim, right_dim):
    return lax.dot_general(
        left_op,
        right_op,
        (((left_dim,), (right_dim,)), ((), ())),
        preferred_element_type=jnp.float32,
    )


def layer_norm(hidden, gain_row, shift_row):
    center = hidden - jnp.mean(hidden, axis=-1, keepdims=True)
    spread = jnp.mean(center * center, axis=-1, keepdims=True)
    return center * lax.rsqrt(spread + EPS_NORM) * gain_row + shift_row


def box_tables(box_rows, model_width):
    quarter = model_width // 4
    frequency = jnp.exp(jnp.arange(quarter).astype(jnp.float32) * (-math.log(10000.0) / quarter))
    angles = box_rows.astype(jnp.float32)[:, :, None] * frequency
    return (jnp.sin(angles), jnp.cos(angles))


def encode(sine_rows, cosine_rows):
    return jnp.concatenate([sine_rows[0], cosine_rows[0], sine_rows[1], cosine_rows[1]], axis=-1)


def rotate(pos_table, sine_rows, cosine_rows):
    quarter = sine_rows.shape[-1]
    pieces = []
    for coord in range(2):
        sine_part = pos_table[..., 2 * coord * quarter : (2 * coord + 1) * quarter]
        cosine_part = pos_table[..., (2 * coord + 1) * quarter : (2 * coord + 2) * quarter]
        pieces.append(cosine_part * sine_rows[coord] - sine_part * cosine_rows[coord])
        pieces.append(sine_part * sine_rows[coord] + cosine_part * cosine_rows[coord])
    return jnp.concatenate(pieces, axis=-1)


def scores(query_rows, key_rows, left_rows, encoded, page_live):
    text_part = jnp.einsum("ihd,jhd->hij", query_rows, key_rows, preferred_element_type=jnp.float32)
    place_part = jnp.einsum("hie,je->hij", left_rows, encoded, preferred_element_type=jnp.float32)
    score_rows = (text_part + place_part) * HEAD_DIM ** (-0.5)
    return jnp.where(page_live[None, None, :], score_rows, MASK_FILL)


def forward_page(weights, token_row_block, box_rows, page_length):
    attention_matrices, up_mat, down_mat, vector_rows = weights
    row_count, model_width = token_row_block.shape
    vector_f32 = vector_rows.astype(jnp.float32)
    page_live = jnp.arange(row_count) < page_length
    projected_rows = jnp.einsum(
        "tb,mby->mty", token_row_block, attention_matrices[:3], preferred_element_type=jnp.float32
    )
    query_rows = (
        (projected_rows[0] + vector_f32[4]).astype(jnp.bfloat16).reshape(row_count, HEADS, HEAD_DIM)
    )
    key_rows = projected_rows[1].astype(jnp.bfloat16).reshape(row_count, HEADS, HEAD_DIM)
    value_rows = (
        (projected_rows[2] + vector_f32[5]).astype(jnp.bfloat16).reshape(row_count, HEADS, HEAD_DIM)
    )
    sine_rows, cosine_rows = box_tables(box_rows, model_width)
    encoded = encode(sine_rows, cosine_rows).astype(jnp.bfloat16)
    rel_heads = attention_matrices[4].reshape(model_width, HEADS, HEAD_DIM)
    pos_table = jnp.einsum(
        "ihd,ehd->hie", query_rows, rel_heads, preferred_element_type=jnp.float32
    )
    left_rows = rotate(pos_table, sine_rows, cosine_rows).astype(jnp.bfloat16)
    score_rows = scores(query_rows, key_rows, left_rows, encoded, page_live)
    row_top = jnp.max(score_rows, axis=-1, keepdims=True)
    exponent = jnp.exp(score_rows - row_top)
    row_total = jnp.sum(exponent, axis=-1, keepdims=True)
    prob_low = (exponent / row_total).astype(jnp.bfloat16)
    logsum = row_top + jnp.log(row_total)
    mixed_rows = jnp.einsum(
        "hij,jhd->ihd", prob_low, value_rows, preferred_element_type=jnp.float32
    )
    context = mixed_rows.reshape(row_count, model_width).astype(jnp.bfloat16)
    attn_out = (
        jnp.dot(context, attention_matrices[3], preferred_element_type=jnp.float32) + vector_f32[6]
    )
    first_sum = token_row_block.astype(jnp.float32) + attn_out
    normed = layer_norm(first_sum, vector_f32[0], vector_f32[1])
    pre_act = jnp.dot(
        normed.astype(jnp.bfloat16), up_mat, preferred_element_type=jnp.float32
    ) + vector_f32[8:].reshape(-1)
    act_low = jax.nn.gelu(pre_act, approximate=False).astype(jnp.bfloat16)
    second_sum = normed + (
        jnp.dot(act_low, down_mat, preferred_element_type=jnp.float32) + vector_f32[7]
    )
    page_out = (layer_norm(second_sum, vector_f32[2], vector_f32[3]) * page_live[:, None]).astype(
        jnp.bfloat16
    )
    saved_state = (
        query_rows,
        key_rows,
        value_rows,
        left_rows,
        logsum,
        context,
        first_sum,
        pre_act,
        act_low,
        second_sum,
    )
    return (page_out, saved_state)


def backward_page(weights, token_row_block, box_rows, page_length, upstream, saved_state):
    attention_matrices, up_mat, down_mat, vector_rows = weights
    (
        query_rows,
        key_rows,
        value_rows,
        left_rows,
        logsum,
        context,
        first_sum,
        pre_act,
        act_low,
        second_sum,
    ) = saved_state
    row_count, model_width = token_row_block.shape
    vector_f32 = vector_rows.astype(jnp.float32)
    page_live = jnp.arange(row_count) < page_length
    sine_rows, cosine_rows = box_tables(box_rows, model_width)
    encoded = encode(sine_rows, cosine_rows).astype(jnp.bfloat16)
    out_grad = upstream.astype(jnp.float32) * page_live[:, None]
    _, pull_second = jax.vjp(layer_norm, second_sum, vector_f32[2], vector_f32[3])
    second_grad, gain_two, shift_two = pull_second(out_grad)
    ffn_grad = second_grad.astype(jnp.bfloat16)
    down_grad = contract(act_low, ffn_grad, 0, 0)
    act_grad = contract(ffn_grad, down_mat, 1, 1)
    _, pull_gelu = jax.vjp(partial(jax.nn.gelu, approximate=False), pre_act)
    pre_grad = pull_gelu(act_grad)[0].astype(jnp.bfloat16)
    normed, pull_first = jax.vjp(layer_norm, first_sum, vector_f32[0], vector_f32[1])
    up_grad = contract(normed.astype(jnp.bfloat16), pre_grad, 0, 0)
    normed_grad = contract(pre_grad, up_mat, 1, 1) + second_grad
    first_grad, gain_one, shift_one = pull_first(normed_grad)
    attn_grad = first_grad.astype(jnp.bfloat16)
    out_mat_grad = contract(context, attn_grad, 0, 0)
    context_grad = (
        contract(attn_grad, attention_matrices[3], 1, 1)
        .astype(jnp.bfloat16)
        .reshape(row_count, HEADS, HEAD_DIM)
    )
    score_rows = scores(query_rows, key_rows, left_rows, encoded, page_live)
    prob_rows = jnp.exp(score_rows - logsum)
    value_grad = jnp.einsum(
        "hij,ihd->jhd",
        prob_rows.astype(jnp.bfloat16),
        context_grad,
        preferred_element_type=jnp.float32,
    ).astype(jnp.bfloat16)
    prob_grad = jnp.einsum(
        "ihd,jhd->hij", context_grad, value_rows, preferred_element_type=jnp.float32
    )
    score_grad = (
        prob_rows * (prob_grad - jnp.sum(prob_rows * prob_grad, axis=-1, keepdims=True))
    ).astype(jnp.bfloat16)
    score_scale = HEAD_DIM ** (-0.5)
    left_grad = (
        jnp.einsum("hij,je->hie", score_grad, encoded, preferred_element_type=jnp.float32)
        * score_scale
    )
    table_grad = rotate(left_grad, sine_rows, cosine_rows).astype(jnp.bfloat16)
    rel_heads = attention_matrices[4].reshape(model_width, HEADS, HEAD_DIM)
    rel_grad = jnp.einsum(
        "hie,ihd->ehd", table_grad, query_rows, preferred_element_type=jnp.float32
    ).reshape(model_width, model_width)
    query_grad = (
        jnp.einsum("hij,jhd->ihd", score_grad, key_rows, preferred_element_type=jnp.float32)
        * score_scale
    )
    query_grad = query_grad + jnp.einsum(
        "hie,ehd->ihd", table_grad, rel_heads, preferred_element_type=jnp.float32
    )
    key_grad = (
        jnp.einsum("hij,ihd->jhd", score_grad, query_rows, preferred_element_type=jnp.float32)
        * score_scale
    )
    stacked_layers = jnp.stack(
        [
            query_grad.astype(jnp.bfloat16).reshape(row_count, model_width),
            key_grad.astype(jnp.bfloat16).reshape(row_count, model_width),
            value_grad.reshape(row_count, model_width),
        ]
    )
    projection_gradient = jnp.einsum(
        "cg,yca->yga", token_row_block, stacked_layers, preferred_element_type=jnp.float32
    )
    token_grad = first_grad + jnp.einsum(
        "skl,scl->kc", stacked_layers, attention_matrices[:3], preferred_element_type=jnp.float32
    )
    column_sums = jnp.sum(stacked_layers.astype(jnp.float32), axis=1)
    attn_grads = jnp.concatenate([projection_gradient, out_mat_grad[None], rel_grad[None]], axis=0)
    small_rows = jnp.stack(
        [
            gain_one,
            shift_one,
            gain_two,
            shift_two,
            column_sums[0],
            column_sums[2],
            jnp.sum(attn_grad.astype(jnp.float32), axis=0),
            jnp.sum(ffn_grad.astype(jnp.float32), axis=0),
        ]
    )
    up_bias_rows = jnp.sum(pre_grad.astype(jnp.float32), axis=0).reshape(-1, model_width)
    vector_grad = jnp.concatenate([small_rows, up_bias_rows], axis=0)
    return (token_grad, (attn_grads, up_grad, down_grad, vector_grad))


def adam_update(weight, first, second, grad, rate, decay_weight):
    first_new = DECAY * first + (1.0 - DECAY) * grad
    second_new = DECAY * second + (1.0 - DECAY) * grad * grad
    correction = 1.0 - DECAY**STEP
    direction = first_new / correction / (jnp.sqrt(second_new / correction) + EPS_ADAM)
    return (weight - rate * (direction + decay_weight * weight), first_new, second_new)


def local(
    tokens,
    boxes,
    lengths,
    cotangent,
    attn_weight,
    up_weight,
    down_weight,
    vectors,
    attn_first,
    up_first,
    down_first,
    vector_first,
    attn_second,
    up_second,
    down_second,
    vector_second,
):
    lowered = (
        attn_weight.astype(jnp.bfloat16),
        up_weight.astype(jnp.bfloat16),
        down_weight.astype(jnp.bfloat16),
        vectors.astype(jnp.bfloat16),
    )
    gathered = (
        lax.all_gather(lowered[0], "fsdp", axis=1, tiled=True),
        lax.all_gather(lowered[1], "fsdp", axis=0, tiled=True),
        lax.all_gather(lowered[2], "fsdp", axis=0, tiled=True),
        lax.all_gather(lowered[3], "fsdp", axis=1, tiled=True),
    )

    def forward_step(carry, page):
        token_row_block, box_rows, page_length = page
        return (carry, forward_page(gathered, token_row_block, box_rows, page_length))

    _, (layer_out, saved_all) = lax.scan(forward_step, None, (tokens, boxes, lengths))
    backward_weights = (
        lax.all_gather(lowered[0], "fsdp", axis=1, tiled=True),
        lax.all_gather(lowered[1], "fsdp", axis=0, tiled=True),
        lax.all_gather(lowered[2], "fsdp", axis=0, tiled=True),
        lax.all_gather(lowered[3], "fsdp", axis=1, tiled=True),
    )
    model_width = gathered[0].shape[2]
    ffn_width = gathered[1].shape[1]
    zero_grads = (
        jnp.zeros((5, model_width, model_width), jnp.float32),
        jnp.zeros((model_width, ffn_width), jnp.float32),
        jnp.zeros((ffn_width, model_width), jnp.float32),
        jnp.zeros(gathered[3].shape, jnp.float32),
    )

    def backward_step(totals, page):
        token_row_block, box_rows, page_length, upstream, saved_state = page
        token_grad, grads = backward_page(
            backward_weights, token_row_block, box_rows, page_length, upstream, saved_state
        )
        return (jax.tree.map(jnp.add, totals, grads), token_grad)

    totals, token_grad = lax.scan(
        backward_step, zero_grads, (tokens, boxes, lengths, cotangent, saved_all)
    )
    shards = (
        lax.psum_scatter(totals[0], "fsdp", scatter_dimension=1, tiled=True),
        lax.psum_scatter(totals[1], "fsdp", scatter_dimension=0, tiled=True),
        lax.psum_scatter(totals[2], "fsdp", scatter_dimension=0, tiled=True),
        lax.psum_scatter(totals[3], "fsdp", scatter_dimension=1, tiled=True),
    )
    reduced = (
        lax.psum(shards[0].astype(jnp.bfloat16), "rep").astype(jnp.float32),
        lax.psum(shards[1].astype(jnp.bfloat16), "rep").astype(jnp.float32),
        lax.psum(shards[2].astype(jnp.bfloat16), "rep").astype(jnp.float32),
        lax.psum(shards[3].astype(jnp.bfloat16), "rep").astype(jnp.float32),
    )
    attn_rates = jnp.array(ATTN_RATES, jnp.float32)[:, None, None]
    attn_new, attn_first_new, attn_second_new = adam_update(
        attn_weight, attn_first, attn_second, reduced[0], attn_rates, WEIGHT_DECAY
    )
    up_new, up_first_new, up_second_new = adam_update(
        up_weight, up_first, up_second, reduced[1], UP_RATE, WEIGHT_DECAY
    )
    down_new, down_first_new, down_second_new = adam_update(
        down_weight, down_first, down_second, reduced[2], DOWN_RATE, WEIGHT_DECAY
    )
    vectors_new, vector_first_new, vector_second_new = adam_update(
        vectors, vector_first, vector_second, reduced[3], VECTOR_RATE, 0.0
    )
    return (
        layer_out,
        token_grad,
        attn_new,
        up_new,
        down_new,
        vectors_new,
        attn_first_new,
        up_first_new,
        down_first_new,
        vector_first_new,
        attn_second_new,
        up_second_new,
        down_second_new,
        vector_second_new,
        attn_new.astype(jnp.bfloat16),
        up_new.astype(jnp.bfloat16),
        down_new.astype(jnp.bfloat16),
        vectors_new.astype(jnp.bfloat16),
    )


def solution(mesh):
    return jax.shard_map(
        local,
        mesh=mesh,
        in_specs=(
            P(("fsdp", "rep"), None, None),
            P(("fsdp", "rep"), None, None),
            P(("fsdp", "rep")),
            P(("fsdp", "rep"), None, None),
            P(None, "fsdp", None),
            P("fsdp", None),
            P("fsdp", None),
            P(None, "fsdp"),
            P(None, "fsdp", None),
            P("fsdp", None),
            P("fsdp", None),
            P(None, "fsdp"),
            P(None, "fsdp", None),
            P("fsdp", None),
            P("fsdp", None),
            P(None, "fsdp"),
        ),
        out_specs=(
            P(("fsdp", "rep"), None, None),
            P(("fsdp", "rep"), None, None),
            P(None, "fsdp", None),
            P("fsdp", None),
            P("fsdp", None),
            P(None, "fsdp"),
            P(None, "fsdp", None),
            P("fsdp", None),
            P("fsdp", None),
            P(None, "fsdp"),
            P(None, "fsdp", None),
            P("fsdp", None),
            P("fsdp", None),
            P(None, "fsdp"),
            P(None, "fsdp", None),
            P("fsdp", None),
            P("fsdp", None),
            P(None, "fsdp"),
        ),
        check_vma=False,
    )
```

profile of v0, /device:TPU:0, one launch (start us, length us, event | category | flops | bytes accessed | tf_op | source)
XLA Modules:
  0.0 1093.8 jit_solution(1731106387310629390)
XLA Ops:
  13.7 43.1 %all-gather = bf16[16,48,12]{1,2,0:T(8,128)(2,1)S(1)} all-gather(bf16[1,48,12]{1,2,0:T(8,128)(2,1)S(1)} %convert_bitcast_fusion.1), channel_id=1, replica_groups=mesh['fsdp'=16,'rep'=2] {'fsdp'}, dimensions={0}, use_global_device_ids=true | all-gather | bytes 19584 | tf_op jit(solution)/shard_map/all_gather | solution.py:272
  64.1 40.9 %all-gather.5.cloned.1.call-done = bf16[5,768,768]{2,1,0:T(8,128)(2,1)} async-done(((bf16[5,48,768]{2,1,0:T(8,128)(2,1)}), bf16[5,768,768]{2,1,0:T(8,128)(2,1)}) %all-gather.5.cloned.1.call-update) | async-done | bytes 5898256 | tf_op jit(solution)/shard_map/all_gather | solution.py:269
  109.9 4.1 convolution_bitcast_fusion.1
  116.2 7.9 fusion.78
  124.3 15.9 %subtract_convert_fusion.3 = (bf16[12,512,192]{2,1,0:T(8,128)(2,1)}, bf16[12,512,192]{2,1,0:T(8,128)(2,1)}, bf16[12,512,192]{2,1,0:T(8,128)(2,1)}, bf16[12,512,192]{2,1,0:T(8,128)(2,1)}) fusion(f32[12,512,768]{2,1,0:T(8,128)} %fusion.78, f32[512,192]{1,0:T(8,128)S(1)} %get-tuple-element.267, f32[512,192]{1,0:T(8,128)S(1)} %copy-done.12, ...), kind=kLoop, calls=%fused_computation.45 | loop fusion | flops 18874368 | bytes 29884416 | tf_op jit(solution)/shard_map/convert.9
  140.2 13.4 %fusion.2 = f32[12,512,512]{1,2,0:T(8,128)} fusion(bf16[12,512,192]{2,1,0:T(8,128)(2,1)} %get-tuple-element.256, bf16[12,512,192]{2,1,0:T(8,128)(2,1)} %get-tuple-element.257, bf16[12,512,192]{2,1,0:T(8,128)(2,1)} %get-tuple-element.251, bf16[12,512,192]{2,1,0:T(8,128)(2,1)} %get-tuple-element.250, bf16[512,192]{1,0:T(8,128)(2,1)S(1)} %copy-done.35, ...), kind=kOutput, calls=%fused_computation.10 | convolution fusion | flops 4872732672 | bytes 22806528 | tf_op jit(solution)/shard_map/while/body/eval_jaxpr/hie,je->hij/dot_general | solution.py:64
  155.0 7.2 fusion.75
  172.7 14.5 %all-gather.7.cloned.1.call-done = bf16[768,3072]{1,0:T(8,128)(2,1)} async-done(((bf16[48,3072]{1,0:T(8,128)(2,1)}), bf16[768,3072]{1,0:T(8,128)(2,1)}) %all-gather.7.cloned.1.call-update) | async-done | bytes 4718608 | tf_op jit(solution)/shard_map/all_gather | solution.py:270
  187.2 20.1 %multiply_convert_fusion.1 = (bf16[512,3072]{1,0:T(8,128)(2,1)}, f32[512,3072]{1,0:T(8,128)}, f32[512,3072]{1,0:T(8,128)}) fusion(f32[3072]{0:T(1024)S(1)} %add.296, bf16[768,3072]{1,0:T(8,128)(2,1)} %all-gather.7.cloned.1.call-done, f32[512,768]{1,0:T(8,128)S(1)} %get-tuple-element.276, f32[768]{0:T(1024)S(1)} %get-tuple-element.210, ...), kind=kOutput, calls=%fused_computation.29 | convolution fusion | flops 2521694208 | bytes 22042624 | tf_op jit(solution)/shard_map/while/body/eval_jaxpr/dot_general | solution.py:106
  207.3 62.4 %all-gather.9.cloned.1.call-done = bf16[3072,768]{1,0:T(8,128)(2,1)} async-done(((bf16[192,768]{1,0:T(8,128)(2,1)}), bf16[3072,768]{1,0:T(8,128)(2,1)}) %all-gather.9.cloned.1.call-update) | async-done | bytes 4718608 | tf_op jit(solution)/shard_map/all_gather | solution.py:271
  269.7 6.2 fusion.77
  280.2 7.0 convert_reduce_fusion
  288.8 5.5 fusion.58
  294.4 8.3 fusion.80
  302.9 6.8 multiply_reduce_fusion.1
  314.2 7.0 fusion.33
  322.4 7.1 multiply_reduce_fusion
  329.5 7.1 multiply_convert_fusion
  344.8 4.5 fusion.79
  349.4 9.4 broadcast_multiply_fusion
  358.9 16.2 %subtract_convert_fusion.1 = (bf16[12,512,192]{2,1,0:T(8,128)(2,1)S(1)}, bf16[12,512,192]{2,1,0:T(8,128)(2,1)}, bf16[12,512,192]{2,1,0:T(8,128)(2,1)}, bf16[12,512,192]{2,1,0:T(8,128)(2,1)}) fusion(f32[12,512,768]{2,1,0:T(8,128)} %broadcast_multiply_fusion, f32[512,192]{1,0:T(8,128)S(1)} %copy-done.8, f32[512,192]{1,0:T(8,128)} %get-tuple-element.284, ...), kind=kLoop, calls=%fused_computation.26 | loop fusion | flops 18874368 | bytes 29884416 | tf_op jit(solution)/shard_map/convert.1
  375.1 9.1 fusion.30
  387.4 4.2 convolution_bitcast_fusion
  392.2 7.5 fusion.45
  399.7 6.4 pad_maximum_fusion
  406.1 16.5 %copy.118 = f32[5,768,768]{2,0,1:T(8,128)} copy(f32[5,768,768]{1,2,0:T(8,128)} %pad_maximum_fusion) | data formatting | bytes 23592960 | tf_op jit(solution)/shard_map/while/body/eval_jaxpr/concatenate | solution.py:218
  426.6 37.6 %reduce-scatter.9.cloned.1.call-done = f32[48,3072]{1,0:T(8,128)} async-done(((f32[768,3072]{1,0:T(8,128)}), f32[48,3072]{1,0:T(8,128)}) %reduce-scatter.9.cloned.1.call-update) | async-done | bytes 589840 | tf_op jit(solution)/shard_map/reduce_scatter | solution.py:307
  465.9 174.6 %reduce-scatter.11.cloned.1.call-done = f32[192,768]{1,0:T(8,128)} async-done(((f32[3072,768]{1,0:T(8,128)}), f32[192,768]{1,0:T(8,128)}) %reduce-scatter.11.cloned.1.call-update) | async-done | bytes 589840 | tf_op jit(solution)/shard_map/reduce_scatter | solution.py:308
  642.3 288.0 %reduce-scatter.7.cloned.1.call-done = f32[5,48,768]{2,0,1:T(8,128)} async-done(((f32[5,768,768]{2,0,1:T(8,128)}), f32[5,48,768]{2,0,1:T(8,128)}) %reduce-scatter.7.cloned.1.call-update) | async-done | bytes 737296 | tf_op jit(solution)/shard_map/reduce_scatter | solution.py:306
  932.6 5.4 fusion.29
  938.0 118.0 %reduce-scatter.13.cloned.1.call-done = f32[48,12]{1,0:T(8,128)} async-done(((f32[768,12]{1,0:T(8,128)}), f32[48,12]{1,0:T(8,128)}) %reduce-scatter.13.cloned.1.call-update) | async-done | bytes 2320
  1060.0 18.7 %all-reduce.3.cloned.1.call-done = (bf16[5,48,768]{2,1,0:T(8,128)(2,1)}, bf16[48,3072]{1,0:T(8,128)(2,1)}, bf16[192,768]{1,0:T(8,128)(2,1)}) async-done(((bf16[5,48,768]{2,1,0:T(8,128)(2,1)}, bf16[48,3072]{1,0:T(8,128)(2,1)}, bf16[192,768]{1,0:T(8,128)(2,1)}), (bf16[5,48,768]{2,1,0:T(8,128)(2,1)}, bf16[48,3072]{1,0:T(8,128)(2,1)}, bf16[192,768]{1,0:T(8,128)(2,1)})) %all-reduce.3.cloned.1.call-update) | async-done | bytes 958480 | tf_op jit(solution)/shard_map/psum | solution.py:312
  (192 shorter events, 77.5 us)
Async XLA Ops:
  7.2 97.8 %all-gather.5.cloned.1.call-start = ((), (), s32[]{:S(2)}) async-start(), calls=%async_computation.4 | async-start | bytes 6266880 | tf_op jit(solution)/shard_map/all_gather | solution.py:269
  9.2 178.1 %all-gather.7.cloned.1.call-start = ((), (), s32[]{:S(2)}) async-start(), calls=%async_computation.5 | async-start | bytes 5013504 | tf_op jit(solution)/shard_map/all_gather | solution.py:270
  11.0 258.7 %all-gather.9.cloned.1.call-start = ((), (), s32[]{:S(2)}) async-start(), calls=%async_computation.6 | async-start | bytes 5013504 | tf_op jit(solution)/shard_map/all_gather | solution.py:271
  12.9 451.2 %reduce-scatter.9.cloned.1.call-start = ((), (), s32[]{:S(2)}) async-start(), calls=%async_computation.8 | async-start | bytes 10027008 | tf_op jit(solution)/shard_map/reduce_scatter | solution.py:307
  61.4 48.5 %copy-start.43 = (bf16[1,512,768]{2,1,0:T(8,128)(2,1)S(1)}, bf16[1,512,768]{2,1,0:T(8,128)(2,1)}, u32[]{:S(2)}) copy-start(bf16[1,512,768]{2,1,0:T(8,128)(2,1)} %param.17) | copy-start | bytes 2359300
  62.3 77.8 %copy-start.31 = (bf16[512,192]{1,0:T(8,128)(2,1)}, bf16[512,192]{1,0:T(8,128)(2,1)S(1)}, u32[]{:S(2)}) copy-start(bf16[512,192]{1,0:T(8,128)(2,1)S(1)} %get-tuple-element.261) | copy-start | bytes 589828
  63.3 60.9 %copy-start.7 = (f32[512,192]{1,0:T(8,128)}, f32[512,192]{1,0:T(8,128)S(1)}, u32[]{:S(2)}) copy-start(f32[512,192]{1,0:T(8,128)S(1)} %get-tuple-element.267) | copy-start | bytes 1179652
  63.3 60.9 %copy-start.9 = (f32[512,192]{1,0:T(8,128)}, f32[512,192]{1,0:T(8,128)S(1)}, u32[]{:S(2)}) copy-start(f32[512,192]{1,0:T(8,128)S(1)} %get-tuple-element.268) | copy-start | bytes 1179652
  63.3 60.9 %copy-start.11 = (f32[512,192]{1,0:T(8,128)}, f32[512,192]{1,0:T(8,128)S(1)}, u32[]{:S(2)}) copy-start(f32[512,192]{1,0:T(8,128)S(1)} %get-tuple-element.283) | copy-start | bytes 1179652
  114.4 49.7 %copy-start.3 = (f32[1,512,768]{1,2,0:T(8,128)}, f32[1,512,768]{1,2,0:T(8,128)S(1)}, u32[]{:S(2)}) copy-start(f32[1,512,768]{1,2,0:T(8,128)S(1)} %get-tuple-element.258) | copy-start | bytes 4718596
  124.2 15.9 %copy-start.33 = (bf16[512,192]{1,0:T(8,128)(2,1)S(1)}, bf16[512,192]{1,0:T(8,128)(2,1)}, u32[]{:S(2)}) copy-start(bf16[512,192]{1,0:T(8,128)(2,1)} %get-tuple-element.262) | copy-start | bytes 589828
  124.2 15.9 %copy-start.35 = (bf16[512,192]{1,0:T(8,128)(2,1)S(1)}, bf16[512,192]{1,0:T(8,128)(2,1)}, u32[]{:S(2)}) copy-start(bf16[512,192]{1,0:T(8,128)(2,1)} %get-tuple-element.285) | copy-start | bytes 589828
  124.2 15.9 %copy-start.37 = (bf16[512,192]{1,0:T(8,128)(2,1)S(1)}, bf16[512,192]{1,0:T(8,128)(2,1)}, u32[]{:S(2)}) copy-start(bf16[512,192]{1,0:T(8,128)(2,1)} %get-tuple-element.286) | copy-start | bytes 589828
  269.7 10.4 slice-start.2
  269.7 10.4 slice-start.4
  269.7 10.4 slice-start.3
  269.7 10.4 slice-start.5
  294.3 346.2 %reduce-scatter.11.cloned.1.call-start = ((), (), s32[]{:S(2)}) async-start(), calls=%async_computation.9 | async-start | bytes 10027008 | tf_op jit(solution)/shard_map/reduce_scatter | solution.py:308
  302.7 627.6 %reduce-scatter.7.cloned.1.call-start = ((), (), s32[]{:S(2)}) async-start(), calls=%async_computation.7 | async-start | bytes 20054016 | tf_op jit(solution)/shard_map/reduce_scatter | solution.py:306
  349.4 9.4 copy-start.10
  358.9 16.2 %copy-start.14 = (bf16[1,768,768]{1,2,0:T(8,128)(2,1)S(1)}, bf16[1,768,768]{1,2,0:T(8,128)(2,1)}, u32[]{:S(2)}) copy-start(bf16[1,768,768]{1,2,0:T(8,128)(2,1)} %copy.105) | copy-start | bytes 3538948
  375.1 10.3 copy-start.24
  422.6 509.9 %copy-start.5 = (f32[512,768]{1,0:T(8,128)S(1)}, f32[512,768]{1,0:T(8,128)}, u32[]{:S(2)}) copy-start(f32[512,768]{1,0:T(8,128)} %copy-done.4) | copy-start | bytes 4718596
  422.6 633.4 %reduce-scatter.13.cloned.1.call-start = ((), (), s32[]{:S(2)}) async-start(), calls=%async_computation.10 | async-start | bytes 417792
  426.5 652.1 %all-reduce.3.cloned.1.call-start = ((), (), s32[]{:S(2)}) async-start(), calls=%async_computation.11 | async-start | bytes 1916928 | tf_op jit(solution)/shard_map/psum | solution.py:312
  932.6 126.8 %copy-start.39 = (f32[12,48]{1,0:T(8,128)S(1)}, f32[12,48]{1,0:T(8,128)}, u32[]{:S(2)}) copy-start(f32[12,48]{1,0:T(8,128)} %param.24) | copy-start | bytes 6916
  932.6 126.8 %copy-start.40 = (f32[12,48]{1,0:T(8,128)S(1)}, f32[12,48]{1,0:T(8,128)}, u32[]{:S(2)}) copy-start(f32[12,48]{1,0:T(8,128)} %param.28) | copy-start | bytes 6916
  932.6 126.7 %copy-start.41 = (f32[12,48]{1,0:T(8,128)S(1)}, f32[12,48]{1,0:T(8,128)}, u32[]{:S(2)}) copy-start(f32[12,48]{1,0:T(8,128)} %param.32) | copy-start | bytes 6916
  938.0 146.8 %copy-start.25 = (f32[5,48,768]{2,1,0:T(8,128)S(1)}, f32[5,48,768]{2,1,0:T(8,128)}, u32[]{:S(2)}) copy-start(f32[5,48,768]{2,1,0:T(8,128)} %param.21) | copy-start | bytes 2211844
  938.0 146.8 %copy-start.28 = (f32[5,48,768]{2,1,0:T(8,128)S(1)}, f32[5,48,768]{2,1,0:T(8,128)}, u32[]{:S(2)}) copy-start(f32[5,48,768]{2,1,0:T(8,128)} %param.25) | copy-start | bytes 2211844
  938.0 146.8 %copy-start.29 = (f32[5,48,768]{2,1,0:T(8,128)S(1)}, f32[5,48,768]{2,1,0:T(8,128)}, u32[]{:S(2)}) copy-start(f32[5,48,768]{2,1,0:T(8,128)} %param.29) | copy-start | bytes 2211844
  938.0 146.8 %copy-start.42 = (f32[5]{0:T(128)S(1)}, f32[5]{0:T(128)}, u32[]{:S(2)}) copy-start(f32[5]{0:T(128)} %constant.297.clone) | copy-start | bytes 64
  (28 other events, 120.2 us)
Sparse Core Ops, SparseCore 0:
  11.3 93.6 all-gather.4
  108.4 78.8 all-gather.6
  190.6 79.0 all-gather.8
  294.4 169.6 reduce-scatter.8
  470.6 169.8 reduce-scatter.10
  646.2 284.1 reduce-scatter.6
  935.5 120.4 reduce-scatter.12
  1059.9 18.6 all-reduce.2
where the time goes:
time: 1100 us; the launch traced here: 1090 us
  waiting for transfers between devices  755 us (69%)
  matrix products  152 us (14%)
  other arithmetic  76.2 us (7%)
  local copies, waits for them, and re-layouts  48.5 us (4%)
  blocking collectives  45.6 us (4%)
  between operations  15.8 us (1%)
    reduce_scatter x1, waiting for transfers between devices, local(): lax.psum_scatter(totals[0], 'fsdp', scatter_dimension=1, tiled=True)  288 us
    reduce_scatter x1, waiting for transfers between devices, local(): lax.psum_scatter(totals[2], 'fsdp', scatter_dimension=0, tiled=True)  175 us
    unnamed x9, waiting for transfers between devices  118 us
    all_gather x1, waiting for transfers between devices, local(): lax.all_gather(lowered[2], 'fsdp', axis=0, tiled=True)  62.4 us
    all_gather x1, blocking collectives, local(): lax.all_gather(lowered[3], 'fsdp', axis=1, tiled=True)  43.1 us
    all_gather x1, waiting for transfers between devices, local(): lax.all_gather(lowered[0], 'fsdp', axis=1, tiled=True)  40.9 us
    reduce_scatter x1, waiting for transfers between devices, local(): lax.psum_scatter(totals[1], 'fsdp', scatter_dimension=0, tiled=True)  37.6 us
    another operation x2, other arithmetic  32.1 us
  transfers between devices with their start and end apart: 8, of which 8 were waited for; matrix products, arithmetic and copies ran while one was open for 21% of the time, Pallas kernels for 0%

commit v1 on v0

--- a/solution.py
+++ b/solution.py
@@ -241,7 +241,193 @@
     return (weight - rate * (direction + decay_weight * weight), first_new, second_new)
 
 
+AXES = ("fsdp", "rep")
+ORDERS = ((8, 4, 2, 1), (8, 4, 1, 2))
+
+
+def mask_table(order):
+    masks = [0]
+    for bit in order:
+        masks = masks + [bit ^ m for m in masks]
+    return masks
+
+
+MASKS = tuple(mask_table(order) for order in ORDERS)
+
+
+def inverse(masks):
+    places = [0] * len(masks)
+    for place, mask in enumerate(masks):
+        places[mask] = place
+    return places
+
+
+PLACES = tuple(inverse(masks) for masks in MASKS)
+
+
+def step_pairs(step):
+    return [
+        (chip * 2 + core, (chip ^ ORDERS[core][step]) * 2 + core)
+        for chip in range(16)
+        for core in range(2)
+    ]
+
+
+CORE_PAIRS = [(chip * 2 + core, chip * 2 + 1 - core) for chip in range(16) for core in range(2)]
+
+
+def swap_cores(block):
+    return lax.ppermute(block, AXES, CORE_PAIRS)
+
+
+def gather_blocks(own_half):
+    held = own_half[None]
+    for step in range(4):
+        held = jnp.concatenate([held, lax.ppermute(held, AXES, step_pairs(step))], axis=0)
+    return held, swap_cores(held)
+
+
+def in_order(mine, other):
+    chip, core = lax.axis_index("fsdp"), lax.axis_index("rep")
+    places = jnp.array(PLACES, jnp.int32)
+    blocks = jnp.arange(16) ^ chip
+    mine = jnp.take(mine, places[core][blocks], axis=0)
+    other = jnp.take(other, places[1 - core][blocks], axis=0)
+    first = jnp.where(core == 0, mine, other)
+    second = jnp.where(core == 0, other, mine)
+    return first, second
+
+
+def scatter_blocks(first, second):
+    chip, core = lax.axis_index("fsdp"), lax.axis_index("rep")
+    masks = jnp.array(MASKS, jnp.int32)
+    keep = jnp.where(core == 0, first, second)
+    send = jnp.where(core == 0, second, first)
+    keep = jnp.take(keep, masks[core] ^ chip, axis=0)
+    send = jnp.take(send, masks[1 - core] ^ chip, axis=0)
+    held = keep + swap_cores(send)
+    for step in (3, 2, 1, 0):
+        half = held.shape[0] // 2
+        held = held[:half] + lax.ppermute(held[half:], AXES, step_pairs(step))
+    mine = held[0]
+    other = swap_cores(mine)
+    first = jnp.where(core == 0, mine, other)
+    second = jnp.where(core == 0, other, mine)
+    return first, second
+
+
 def local(
+    tokens,
+    boxes,
+    lengths,
+    cotangent,
+    attn_weight,
+    up_weight,
+    down_weight,
+    vectors,
+    attn_first,
+    up_first,
+    down_first,
+    vector_first,
+    attn_second,
+    up_second,
+    down_second,
+    vector_second,
+):
+    core = lax.axis_index("rep")
+    attn_low = attn_weight.astype(jnp.bfloat16)
+    up_low = up_weight.astype(jnp.bfloat16).reshape(48, 4, 768).transpose(1, 0, 2)
+    down_low = down_weight.astype(jnp.bfloat16).reshape(4, 48, 768)
+    vec_low = jnp.pad(vectors.astype(jnp.bfloat16), ((0, 4), (0, 768 - 48)))
+    halves_one = jnp.stack([
+        jnp.concatenate([attn_low[0], attn_low[1], vec_low]),
+        jnp.concatenate([attn_low[2], attn_low[4], vec_low]),
+    ])
+    halves_two = jnp.stack([
+        jnp.concatenate([attn_low[3, :, :384].reshape(24, 768), up_low[0], up_low[1]]),
+        jnp.concatenate([attn_low[3, :, 384:].reshape(24, 768), up_low[2], up_low[3]]),
+    ])
+    halves_three = jnp.stack([
+        jnp.concatenate([down_low[0], down_low[1]]),
+        jnp.concatenate([down_low[2], down_low[3]]),
+    ])
+    def own(halves):
+        return lax.dynamic_index_in_dim(halves, core, 0, keepdims=False)
+    one = in_order(*gather_blocks(own(halves_one)))
+    two = in_order(*gather_blocks(own(halves_two)))
+    three = in_order(*gather_blocks(own(halves_three)))
+    def square(piece, start):
+        return piece[:, start:start + 48].reshape(768, 768)
+    w_o = jnp.concatenate([p[:, :24].reshape(768, 384) for p in two], axis=1)
+    attn_full = jnp.stack([square(one[0], 0), square(one[0], 48), square(one[1], 0), w_o, square(one[1], 48)])
+    up_full = jnp.concatenate([square(p, 24 + 48 * i) for p in two for i in range(2)], axis=1)
+    down_full = jnp.concatenate(three, axis=1).reshape(3072, 768)
+    vec_full = one[0][:, 96:108, :48].transpose(1, 0, 2).reshape(12, 768)
+    weights = (attn_full, up_full, down_full, vec_full)
+    page_out, saved_state = forward_page(weights, tokens[0], boxes[0], lengths[0])
+    layer_out = page_out[None]
+    token_grad, (attn_grads, up_grad, down_grad, vector_grad) = backward_page(
+        weights, tokens[0], boxes[0], lengths[0], cotangent[0], saved_state
+    )
+    token_grad = token_grad[None]
+    def low(v):
+        return v.astype(jnp.bfloat16)
+    down_blocks = low(down_grad).reshape(16, 192, 768)
+    three = scatter_blocks(down_blocks[:, :96], down_blocks[:, 96:])
+    up_blocks = low(up_grad).reshape(16, 48, 4, 768).transpose(0, 2, 1, 3)
+    attn_blocks = low(attn_grads).reshape(5, 16, 48, 768)
+    o_blocks = attn_blocks[3]
+    two = scatter_blocks(
+        *(jnp.concatenate([o_blocks[:, :, 384 * i:384 * i + 384].reshape(16, 24, 768), up_blocks[:, 2 * i], up_blocks[:, 2 * i + 1]], axis=1)
+        for i in range(2)))
+    vec_blocks = jnp.pad(low(vector_grad).reshape(12, 16, 48).transpose(1, 0, 2), ((0, 0), (0, 4), (0, 720)))
+    one = scatter_blocks(
+        jnp.concatenate([attn_blocks[0], attn_blocks[1], vec_blocks], axis=1),
+        jnp.concatenate([attn_blocks[2], attn_blocks[4], vec_blocks], axis=1))
+    wide = [v.astype(jnp.float32) for v in (*one, *two, *three)]
+    o_sum = jnp.concatenate([wide[2][:24].reshape(48, 384), wide[3][:24].reshape(48, 384)], axis=1)
+    reduced = (
+        jnp.stack([wide[0][:48], wide[0][48:96], wide[1][:48], o_sum, wide[1][48:96]]),
+        jnp.concatenate([wide[2][24:72], wide[2][72:], wide[3][24:72], wide[3][72:]], axis=1),
+        jnp.concatenate([wide[4], wide[5]], axis=0),
+        wide[0][96:108, :48],
+    )
+    attn_rates = jnp.array(ATTN_RATES, jnp.float32)[:, None, None]
+    attn_new, attn_first_new, attn_second_new = adam_update(
+        attn_weight, attn_first, attn_second, reduced[0], attn_rates, WEIGHT_DECAY
+    )
+    up_new, up_first_new, up_second_new = adam_update(
+        up_weight, up_first, up_second, reduced[1], UP_RATE, WEIGHT_DECAY
+    )
+    down_new, down_first_new, down_second_new = adam_update(
+        down_weight, down_first, down_second, reduced[2], DOWN_RATE, WEIGHT_DECAY
+    )
+    vectors_new, vector_first_new, vector_second_new = adam_update(
+        vectors, vector_first, vector_second, reduced[3], VECTOR_RATE, 0.0
+    )
+    return (
+        layer_out,
+        token_grad,
+        attn_new,
+        up_new,
+        down_new,
+        vectors_new,
+        attn_first_new,
+        up_first_new,
+        down_first_new,
+        vector_first_new,
+        attn_second_new,
+        up_second_new,
+        down_second_new,
+        vector_second_new,
+        attn_new.astype(jnp.bfloat16),
+        up_new.astype(jnp.bfloat16),
+        down_new.astype(jnp.bfloat16),
+        vectors_new.astype(jnp.bfloat16),
+    )
+
+
+def local_general(
     tokens,
     boxes,
     lengths,
@@ -350,8 +536,9 @@
 
 
 def solution(mesh):
+    blocked = mesh.shape["fsdp"] == 16 and mesh.shape["rep"] == 2
     return jax.shard_map(
-        local,
+        local if blocked else local_general,
         mesh=mesh,
         in_specs=(
             P(("fsdp", "rep"), None, None),

time: 1100 us -> 555 us (0.50)
  waiting for transfers between devices: 755 us -> 107 us
  local copies, waits for them, and re-layouts: 48.5 us -> 133 us
  other arithmetic: 76.2 us -> 123 us
  blocking collectives: 45.6 us -> 0 us
  starting transfers between devices: 0.5 us -> 34.6 us
  between operations: 15.8 us -> 3.26 us
    reduce_scatter x3 -> x0, waiting for transfers between devices: 500 us -> none  [the longest x1 288 us: local(): lax.psum_scatter(totals[0], 'fsdp', scatter_dimension=1, tiled=True)]
    unnamed x9 -> x0, waiting for transfers between devices: 118 us -> none
    all_gather x3 -> x0, waiting for transfers between devices: 118 us -> none  [the longest x1 62.4 us: local(): lax.all_gather(lowered[2], 'fsdp', axis=0, tiled=True)]
    ppermute x0 -> x33, waiting for transfers between devices: none -> 107 us  [the longest x12 55.1 us: scatter_blocks(): held = held[:half] + lax.ppermute(held[half:], AXES, step_pairs(step))]
    gather x0 -> x14, local copies, waits for them, and re-layouts: none -> 43.3 us  [the longest x4 12.6 us: in_order(): other = jnp.take(other, places[1 - core][blocks], axis=0)]
    all_gather x1 -> x0, blocking collectives: 43.1 us -> none  [local(): lax.all_gather(lowered[3], 'fsdp', axis=1, tiled=True)]
    ppermute x0 -> x33, starting transfers between devices: none -> 34.6 us  [the longest x12 16.9 us: gather_blocks(): lax.ppermute(held, AXES, step_pairs(step))]
    select_n x0 -> x13, other arithmetic: none -> 29.1 us  [the longest x3 11.2 us: scatter_blocks(): keep = jnp.where(core == 0, first, second)]
  transfers between devices with their start and end apart: 8 -> 33, of which waited for: 8 -> 22; matrix products, arithmetic and copies ran while one was open for 21% -> 38% of each run, Pallas kernels for 0% -> 0%
where the time goes in v1:
time: 555 us; the launch traced here: 545 us
  matrix products  144 us (26%)
  local copies, waits for them, and re-layouts  133 us (24%)
  other arithmetic  123 us (22%)
  waiting for transfers between devices  107 us (19%)
  starting transfers between devices  34.6 us (6%)
    ppermute x12, waiting for transfers between devices, scatter_blocks(): held = held[:half] + lax.ppermute(held[half:], AXES, step_pairs(step))  55.1 us
    ppermute x12, waiting for transfers between devices, gather_blocks(): lax.ppermute(held, AXES, step_pairs(step))  50.4 us
    another operation x2, other arithmetic  30.5 us
    dot_general x6, matrix products, contract(): lax.dot_general(left_op, right_op, (((left_dim,), (right_dim,)), ((), ())...  26.2 us
    dot_general x1, matrix products, forward_page(): jnp.dot(normed.astype(jnp.bfloat16), up_mat, preferred_element_type=jnp.f...  20.5 us
    ppermute x12, starting transfers between devices, gather_blocks(): lax.ppermute(held, AXES, step_pairs(step))  16.9 us
    ppermute x12, starting transfers between devices, scatter_blocks(): held = held[:half] + lax.ppermute(held[half:], AXES, step_pairs(step))  16.5 us
    unnamed x191, local copies, waits for them, and re-layouts  16.5 us
  transfers between devices with their start and end apart: 33, of which 22 were waited for; matrix products, arithmetic and copies ran while one was open for 38% of the time, Pallas kernels for 0%

profile of v1, /device:TPU:0, one launch (start us, length us, event | category | flops | bytes accessed | tf_op | source)
XLA Modules:
  0.0 545.0 jit_solution(12278100991892974792)
XLA Ops:
  13.9 8.6 %collective-permute-done.10 = bf16[1,96,768]{2,1,0:T(8,128)(2,1)} collective-permute-done((bf16[1,96,768]{2,1,0:T(8,128)(2,1)}, bf16[1,96,768]{2,1,0:T(8,128)(2,1)}, u32[]{:S(2)}, u32[]{:S(2)}) %collective-permute-start.10) | collective-permute-done | bytes 147488 | tf_op jit(solution)/shard_map/ppermute | solution.py:286
  29.0 6.7 %collective-permute-done.11 = bf16[2,96,768]{2,1,0:T(8,128)(2,1)} collective-permute-done((bf16[2,96,768]{2,1,0:T(8,128)(2,1)}, bf16[2,96,768]{2,1,0:T(8,128)(2,1)}, u32[]{:S(2)}, u32[]{:S(2)}) %collective-permute-start.11) | collective-permute-done | bytes 294944 | tf_op jit(solution)/shard_map/ppermute | solution.py:286
  38.5 4.4 collective-permute-done.1
  49.6 10.7 %collective-permute-done.2 = bf16[4,112,768]{2,1,0:T(8,128)(2,1)S(1)} collective-permute-done((bf16[4,112,768]{2,1,0:T(8,128)(2,1)S(1)}, bf16[4,112,768]{2,1,0:T(8,128)(2,1)S(1)}, u32[]{:S(2)}, u32[]{:S(2)}) %collective-permute-start.2) | collective-permute-done | bytes 688160 | tf_op jit(solution)/shard_map/ppermute | solution.py:286
  77.4 12.0 %collective-permute-done.3 = bf16[8,112,768]{2,1,0:T(8,128)(2,1)S(1)} collective-permute-done((bf16[8,112,768]{2,1,0:T(8,128)(2,1)S(1)}, bf16[8,112,768]{2,1,0:T(8,128)(2,1)S(1)}, u32[]{:S(2)}, u32[]{:S(2)}) %collective-permute-start.3) | collective-permute-done | bytes 1376288 | tf_op jit(solution)/shard_map/ppermute | solution.py:286
  157.5 7.9 %fusion.118 = f32[12,512,768]{2,1,0:T(8,128)} fusion(bf16[512,12,64]{0,2,1:T(8,128)(2,1)S(1)} %add_convert_fusion.6, bf16[768,12,64]{0,2,1:T(8,128)(2,1)S(1)} %copy-done.15), kind=kOutput, calls=%fused_computation.339 | convolution fusion | flops 603979776 | bytes 20840448 | tf_op jit(solution)/shard_map/ihd,ehd->hie/dot_general | solution.py:87
  165.4 15.4 %subtract_convert_fusion.3 = (bf16[12,512,192]{2,1,0:T(8,128)(2,1)S(1)}, bf16[12,512,192]{2,1,0:T(8,128)(2,1)}, bf16[12,512,192]{2,1,0:T(8,128)(2,1)}, bf16[12,512,192]{2,1,0:T(8,128)(2,1)}) fusion(f32[12,512,768]{2,1,0:T(8,128)} %fusion.118, f32[512,192]{1,0:T(8,128)S(1)} %copy-done.10, f32[512,192]{1,0:T(8,128)S(1)} %copy-done.14, ...), kind=kLoop, calls=%fused_computation.57 | loop fusion | flops 18874368 | bytes 29884416 | tf_op jit(solution)/shard_map/convert.38
  180.9 13.2 %fusion.2 = f32[12,512,512]{1,2,0:T(8,128)} fusion(bf16[12,512,192]{2,1,0:T(8,128)(2,1)} %get-tuple-element.85, bf16[12,512,192]{2,1,0:T(8,128)(2,1)} %get-tuple-element.86, bf16[12,512,192]{2,1,0:T(8,128)(2,1)} %get-tuple-element.80, bf16[12,512,192]{2,1,0:T(8,128)(2,1)S(1)} %get-tuple-element.79, bf16[512,192]{1,0:T(8,128)(2,1)S(1)} %copy-done.64, ...), kind=kOutput, calls=%fused_computation.23 | convolution fusion | flops 4872732672 | bytes 22806528 | tf_op jit(solution)/shard_map/hie,je->hij/dot_general | solution.py:64
  194.1 9.1 %fusion.115 = (f32[12,512]{1,0:T(8,128)S(1)}, f32[12,512,512]{1,2,0:T(8,128)}) fusion(f32[12,512,512]{1,2,0:T(8,128)} %fusion.2, bf16[512,12,64]{0,2,1:T(8,128)(2,1)S(1)} %add_convert_fusion.6, bf16[512,12,64]{0,2,1:T(8,128)(2,1)S(1)} %bitcast.200, pred[512]{0:T(512)(128)(4,1)S(1)} %get-tuple-element.179), kind=kOutput, calls=%fused_computation.336 | convolution fusion | flops 415229952 | bytes 26763776 | tf_op jit(solution)/shard_map/ihd,jhd->hij/dot_general | solution.py:63
  203.8 6.6 %fusion = f32[12,512]{1,0:T(8,128)S(1)} fusion(f32[12,512,512]{1,2,0:T(8,128)} %get-tuple-element.158, f32[12,512]{1,0:T(8,128)S(1)} %get-tuple-element.157), kind=kLoop, calls=%fused_computation.20 | loop fusion | flops 6285312 | bytes 12632064 | tf_op jit(solution)/shard_map/reduce_sum | solution.py:94
  231.3 20.5 %multiply_convert_fusion.1 = (bf16[512,3072]{1,0:T(8,128)(2,1)S(1)}, f32[512,3072]{1,0:T(8,128)}, f32[512,3072]{1,0:T(8,128)}) fusion(f32[3072]{0:T(1024)S(1)} %add.314, bf16[768,768]{1,0:T(8,128)(2,1)} %bitcast.228, bf16[768,768]{1,0:T(8,128)(2,1)S(1)} %bitcast.226, bf16[768,768]{1,0:T(8,128)(2,1)S(1)} %bitcast.224, bf16[768,768]{1,0:T(8,128)(2,1)S(1)} %bitcast.222, ...), kind=kOutput, calls=%fused_computation.41 | convolution fusion | flops 2540568576 | bytes 22042624 | tf_op jit(solution)/shard_map/dot_general | solution.py:106
  257.8 8.9 %fusion.95 = (bf16[3072]{0:T(1024)(128)(2,1)S(1)}, bf16[512,3072]{1,0:T(8,128)(2,1)}) fusion(f32[512,3072]{1,0:T(8,128)} %get-tuple-element.70, f32[512,3072]{1,0:T(8,128)} %get-tuple-element.161, f32[3072]{0:T(1024)S(1)} %add.314, bf16[512,768]{1,0:T(8,128)(2,1)S(1)} %get-tuple-element.60, bf16[3072,768]{1,0:T(8,128)(2,1)S(1)} %bitcast.213), kind=kOutput, calls=%fused_computation.320 | convolution fusion | flops 2441081856 | bytes 21252096 | tf_op jit(solution)/shard_map/dot_general | solution.py:26
  266.7 5.2 multiply_reduce_fusion.1
  271.9 4.8 convolution_convert_fusion.1
  281.0 4.7 convolution_convert_fusion
  286.0 7.7 %fusion.32 = bf16[12,64,512]{2,1,0:T(8,128)(2,1)} fusion(bf16[512,12,64]{0,2,1:T(8,128)(2,1)S(1)} %bitcast.202, f32[12,512,512]{1,2,0:T(8,128)} %get-tuple-element.158, f32[12,512]{1,0:T(8,128)S(1)} %log_add_fusion), kind=kOutput, calls=%fused_computation.135 | convolution fusion | flops 409337856 | bytes 14180352 | tf_op jit(solution)/shard_map/hij,ihd->jhd/dot_general | solution.py:171
  293.7 8.9 %multiply_reduce_fusion = (f32[12,512]{1,0:T(8,128)S(1)}, f32[12,512,512]{1,2,0:T(8,128)}) fusion(f32[12,512,512]{1,2,0:T(8,128)} %get-tuple-element.158, f32[12,512]{1,0:T(8,128)S(1)} %log_add_fusion, bf16[512,12,64]{0,2,1:T(8,128)(2,1)S(1)} %bitcast.203, f32[512,12,64]{0,2,1:T(8,128)S(1)} %bitcast.205, f32[12,64]{1,0:T(8,128)S(1)} %add.297), kind=kOutput, calls=%fused_computation.15 | convolution fusion | flops 412870656 | bytes 27577344 | tf_op jit(solution)/shard_map/ihd,jhd->hij/dot_general | solution.py:177
  302.6 6.9 %multiply_convert_fusion = bf16[12,512,512]{1,2,0:T(8,128)(2,1)S(1)} fusion(f32[12,512,512]{1,2,0:T(8,128)} %get-tuple-element.166, f32[12,512,512]{1,2,0:T(8,128)S(1)} %bitcast.198, f32[12,512]{1,0:T(8,128)S(1)} %get-tuple-element.165, f32[12,512]{1,0:T(8,128)S(1)} %log_add_fusion), kind=kLoop, calls=%fused_computation.14 | loop fusion | flops 12582912 | bytes 31506432 | tf_op jit(solution)/shard_map/convert_element_type | solution.py:182
  313.7 9.3 %broadcast_multiply_fusion = f32[12,512,768]{2,1,0:T(8,128)} fusion(bf16[12,512,512]{1,2,0:T(8,128)(2,1)S(1)} %multiply_convert_fusion, bf16[512,192]{1,0:T(8,128)(2,1)S(1)} %copy-done.65, bf16[512,192]{1,0:T(8,128)(2,1)S(1)} %copy-done.63, bf16[512,192]{1,0:T(8,128)(2,1)S(1)} %copy-done.67, bf16[512,192]{1,0:T(8,128)(2,1)S(1)} %copy-done.61), kind=kOutput, calls=%fused_computation.32 | convolution fusion | flops 4839702528 | bytes 25952256 | tf_op jit(solution)/shard_map/hij,je->hie/dot_general | solution.py:185
  327.7 15.1 %subtract_convert_fusion.1 = (bf16[12,512,192]{2,1,0:T(8,128)(2,1)S(1)}, bf16[12,512,192]{2,1,0:T(8,128)(2,1)S(1)}, bf16[12,512,192]{2,1,0:T(8,128)(2,1)}, bf16[12,512,192]{2,1,0:T(8,128)(2,1)}) fusion(f32[12,512,768]{2,1,0:T(8,128)} %broadcast_multiply_fusion, f32[512,192]{1,0:T(8,128)S(1)} %copy-done.11, f32[512,192]{1,0:T(8,128)} %get-tuple-element.176, ...), kind=kLoop, calls=%fused_computation.38 | loop fusion | flops 18874368 | bytes 29884416 | tf_op jit(solution)/shard_map/convert.30
  342.8 8.0 %fusion.31 = bf16[768,12,64]{0,2,1:T(8,128)(2,1)} fusion(bf16[512,12,64]{0,2,1:T(8,128)(2,1)S(1)} %add_convert_fusion.6, bf16[12,512,192]{2,1,0:T(8,128)(2,1)} %get-tuple-element.83, bf16[12,512,192]{2,1,0:T(8,128)(2,1)} %get-tuple-element.84, bf16[12,512,192]{2,1,0:T(8,128)(2,1)S(1)} %get-tuple-element.76, bf16[12,512,192]{2,1,0:T(8,128)(2,1)S(1)} %get-tuple-element.75), kind=kOutput, calls=%fused_computation.134 | convolution fusion | flops 642318336 | bytes 11403264 | tf_op jit(solution)/shard_map/hie,ihd->ehd/dot_general | solution.py:190
  350.7 8.0 %add_convert_fusion.5 = bf16[12,64,512]{2,1,0:T(8,128)(2,1)} fusion(f32[12,64,512]{2,1,0:T(8,128)S(1)} %fusion.119, bf16[768,12,64]{0,2,1:T(8,128)(2,1)S(1)} %copy-done.16, bf16[12,512,192]{2,1,0:T(8,128)(2,1)} %get-tuple-element.83, bf16[12,512,192]{2,1,0:T(8,128)(2,1)} %get-tuple-element.84, bf16[12,512,192]{2,1,0:T(8,128)(2,1)S(1)} %get-tuple-element.76, ...), kind=kOutput, calls=%fused_computation.114 | convolution fusion | flops 642908160 | bytes 12976128 | tf_op jit(solution)/shard_map/hie,ehd->ihd/dot_general | solution.py:197
  360.7 5.0 convert_bitcast_fusion
  365.9 10.0 %reshape.319 = bf16[16,48,4,768]{3,2,1,0:T(4,128)(2,1)} reshape(bf16[768,3072]{1,0:T(8,128)(2,1)} %convolution_convert_fusion.1) | data formatting | bytes 9437184 | tf_op jit(solution)/shard_map/reshape | solution.py:377
  375.9 5.2 copy.225
  381.5 4.8 broadcast_select_fusion.18
  395.2 4.7 reshape.477
  447.9 6.2 %collective-permute-done.28 = bf16[8,96,768]{2,1,0:T(8,128)(2,1)} collective-permute-done((bf16[8,96,768]{2,1,0:T(8,128)(2,1)}, bf16[8,96,768]{2,1,0:T(8,128)(2,1)}, u32[]{:S(2)}, u32[]{:S(2)}) %collective-permute-start.28) | collective-permute-done | bytes 1179680 | tf_op jit(solution)/shard_map/ppermute | solution.py:311
  465.7 7.6 %collective-permute-done.29 = bf16[4,96,768]{2,1,0:T(8,128)(2,1)S(1)} collective-permute-done((bf16[4,96,768]{2,1,0:T(8,128)(2,1)}, bf16[4,96,768]{2,1,0:T(8,128)(2,1)S(1)}, u32[]{:S(2)}, u32[]{:S(2)}) %collective-permute-start.29) | collective-permute-done | bytes 589856 | tf_op jit(solution)/shard_map/ppermute | solution.py:311
  488.7 6.8 %collective-permute-done.17 = bf16[4,112,768]{2,1,0:T(8,128)(2,1)S(1)} collective-permute-done((bf16[4,112,768]{2,1,0:T(8,128)(2,1)S(1)}, bf16[4,112,768]{2,1,0:T(8,128)(2,1)S(1)}, u32[]{:S(2)}, u32[]{:S(2)}) %collective-permute-start.17) | collective-permute-done | bytes 688160 | tf_op jit(solution)/shard_map/ppermute | solution.py:311
  513.5 9.7 %collective-permute-done.24 = bf16[2,120,768]{2,1,0:T(8,128)(2,1)S(1)} collective-permute-done((bf16[2,120,768]{2,1,0:T(8,128)(2,1)S(1)}, bf16[2,120,768]{2,1,0:T(8,128)(2,1)S(1)}, u32[]{:S(2)}, u32[]{:S(2)}) %collective-permute-start.24) | collective-permute-done | bytes 368672 | tf_op jit(solution)/shard_map/ppermute | solution.py:311
  525.6 8.9 %collective-permute-done.25 = bf16[1,120,768]{2,1,0:T(8,128)(2,1)S(1)} collective-permute-done((bf16[1,120,768]{2,1,0:T(8,128)(2,1)S(1)}, bf16[1,120,768]{2,1,0:T(8,128)(2,1)S(1)}, u32[]{:S(2)}, u32[]{:S(2)}) %collective-permute-start.25) | collective-permute-done | bytes 184352 | tf_op jit(solution)/shard_map/ppermute | solution.py:311
  (437 shorter events, 270.5 us)
Async XLA Ops:
  2.6 19.8 %collective-permute-start.10 = (bf16[1,96,768]{2,1,0:T(8,128)(2,1)}, bf16[1,96,768]{2,1,0:T(8,128)(2,1)}, u32[]{:S(2)}, u32[]{:S(2)}) collective-permute-start(bf16[1,96,768]{2,1,0:T(8,128)(2,1)} %get-tuple-element.68), channel_id=1, source_target_pairs={{0,16},{1,17},{2,18},{3,19},{4,20},{5,21},{6,22},{7,23},{8,24},{9,... | collective-permute-start | bytes 442376 | tf_op jit(solution)/shard_map/ppermute | solution.py:286
  9.3 16.8 %collective-permute-start = (bf16[1,112,768]{2,1,0:T(8,128)(2,1)S(1)}, bf16[1,112,768]{2,1,0:T(8,128)(2,1)S(1)}, u32[]{:S(2)}, u32[]{:S(2)}) collective-permute-start(bf16[1,112,768]{2,1,0:T(8,128)(2,1)S(1)} %get-tuple-element.72), channel_id=1, source_target_pairs={{0,16},{1,17},{2,18},{3,19},{4,20},{5,21},{6,22},{7,23},{8,24},{9,... | collective-permute-start | bytes 516104 | tf_op jit(solution)/shard_map/ppermute | solution.py:286
  11.0 52.4 %collective-permute-start.5 = (bf16[1,120,768]{2,1,0:T(8,128)(2,1)}, bf16[1,120,768]{2,1,0:T(8,128)(2,1)S(1)}, u32[]{:S(2)}, u32[]{:S(2)}) collective-permute-start(bf16[1,120,768]{2,1,0:T(8,128)(2,1)} %get-tuple-element.74), channel_id=1, source_target_pairs={{0,16},{1,17},{2,18},{3,19},{4,20},{5,21},{6,22},{7,23},{8,24},{9,... | collective-permute-start | bytes 552968 | tf_op jit(solution)/shard_map/ppermute | solution.py:286
  24.2 11.5 %collective-permute-start.11 = (bf16[2,96,768]{2,1,0:T(8,128)(2,1)}, bf16[2,96,768]{2,1,0:T(8,128)(2,1)}, u32[]{:S(2)}, u32[]{:S(2)}) collective-permute-start(bf16[2,96,768]{2,1,0:T(8,128)(2,1)} %pad_maximum_fusion.20), channel_id=1, source_target_pairs={{0,8},{1,9},{2,10},{3,11},{4,12},{5,13},{6,14},{7,15},{8,0},{9,1},... | collective-permute-start | bytes 884744 | tf_op jit(solution)/shard_map/ppermute | solution.py:286
  27.6 15.3 %collective-permute-start.1 = (bf16[2,112,768]{2,1,0:T(8,128)(2,1)}, bf16[2,112,768]{2,1,0:T(8,128)(2,1)S(1)}, u32[]{:S(2)}, u32[]{:S(2)}) collective-permute-start(bf16[2,112,768]{2,1,0:T(8,128)(2,1)} %pad_maximum_fusion.19), channel_id=1, source_target_pairs={{0,8},{1,9},{2,10},{3,11},{4,12},{5,13},{6,14},{7,15},{8,0},{9,1},... | collective-permute-start | bytes 1032200 | tf_op jit(solution)/shard_map/ppermute | solution.py:286
  36.8 9.9 %collective-permute-start.12 = (bf16[4,96,768]{2,1,0:T(8,128)(2,1)S(1)}, bf16[4,96,768]{2,1,0:T(8,128)(2,1)S(1)}, u32[]{:S(2)}, u32[]{:S(2)}) collective-permute-start(bf16[4,96,768]{2,1,0:T(8,128)(2,1)S(1)} %pad_maximum_fusion.16), channel_id=1, source_target_pairs={{0,4},{1,3},{2,6},{3,1},{4,0},{5,7},{6,2},{7,5},{8,12},{9,11},{10,... | collective-permute-start | bytes 1769480 | tf_op jit(solution)/shard_map/ppermute | solution.py:286
  44.1 16.2 %collective-permute-start.2 = (bf16[4,112,768]{2,1,0:T(8,128)(2,1)S(1)}, bf16[4,112,768]{2,1,0:T(8,128)(2,1)S(1)}, u32[]{:S(2)}, u32[]{:S(2)}) collective-permute-start(bf16[4,112,768]{2,1,0:T(8,128)(2,1)S(1)} %pad_maximum_fusion.15), channel_id=1, source_target_pairs={{0,4},{1,3},{2,6},{3,1},{4,0},{5,7},{6,2},{7,5},{8,12},{9,11},{10,... | collective-permute-start | bytes 2064392 | tf_op jit(solution)/shard_map/ppermute | solution.py:286
  48.0 27.4 %collective-permute-start.13 = (bf16[8,96,768]{2,1,0:T(8,128)(2,1)S(1)}, bf16[8,96,768]{2,1,0:T(8,128)(2,1)S(1)}, u32[]{:S(2)}, u32[]{:S(2)}) collective-permute-start(bf16[8,96,768]{2,1,0:T(8,128)(2,1)S(1)} %pad_maximum_fusion.11), channel_id=1, source_target_pairs={{0,2},{1,5},{2,0},{3,7},{4,6},{5,1},{6,4},{7,3},{8,10},{9,13},{10,... | collective-permute-start | bytes 3538952 | tf_op jit(solution)/shard_map/ppermute | solution.py:286
  60.4 29.0 %collective-permute-start.3 = (bf16[8,112,768]{2,1,0:T(8,128)(2,1)S(1)}, bf16[8,112,768]{2,1,0:T(8,128)(2,1)S(1)}, u32[]{:S(2)}, u32[]{:S(2)}) collective-permute-start(bf16[8,112,768]{2,1,0:T(8,128)(2,1)S(1)} %pad_maximum_fusion.10), channel_id=1, source_target_pairs={{0,2},{1,5},{2,0},{3,7},{4,6},{5,1},{6,4},{7,3},{8,10},{9,13},{10,... | collective-permute-start | bytes 4128776 | tf_op jit(solution)/shard_map/ppermute | solution.py:286
  64.4 7.6 %collective-permute-start.6 = (bf16[2,120,768]{2,1,0:T(8,128)(2,1)S(1)}, bf16[2,120,768]{2,1,0:T(8,128)(2,1)S(1)}, u32[]{:S(2)}, u32[]{:S(2)}) collective-permute-start(bf16[2,120,768]{2,1,0:T(8,128)(2,1)S(1)} %pad_maximum_fusion.18), channel_id=1, source_target_pairs={{0,8},{1,9},{2,10},{3,11},{4,12},{5,13},{6,14},{7,15},{8,0},{9,1},... | collective-permute-start | bytes 1105928 | tf_op jit(solution)/shard_map/ppermute | solution.py:286
  73.0 18.2 %collective-permute-start.7 = (bf16[4,120,768]{2,1,0:T(8,128)(2,1)S(1)}, bf16[4,120,768]{2,1,0:T(8,128)(2,1)S(1)}, u32[]{:S(2)}, u32[]{:S(2)}) collective-permute-start(bf16[4,120,768]{2,1,0:T(8,128)(2,1)S(1)} %pad_maximum_fusion.14), channel_id=1, source_target_pairs={{0,4},{1,3},{2,6},{3,1},{4,0},{5,7},{6,2},{7,5},{8,12},{9,11},{10,... | collective-permute-start | bytes 2211848 | tf_op jit(solution)/shard_map/ppermute | solution.py:286
  76.5 44.2 %collective-permute-start.14 = (bf16[16,96,768]{2,1,0:T(8,128)(2,1)}, bf16[16,96,768]{2,1,0:T(8,128)(2,1)}, u32[]{:S(2)}, u32[]{:S(2)}) collective-permute-start(bf16[16,96,768]{2,1,0:T(8,128)(2,1)} %constant_dynamic-update-slice_fusion.12), channel_id=1, source_target_pairs={{0,1},{1,0},{2,3},{3,2},{4,5},{5,4},{6,7},{7,6},{8,9},{9,8},{10,11... | collective-permute-start | bytes 7077896 | tf_op jit(solution)/shard_map/ppermute | solution.py:280
  90.6 39.4 %collective-permute-start.4 = (bf16[16,112,768]{2,1,0:T(8,128)(2,1)}, bf16[16,112,768]{2,1,0:T(8,128)(2,1)}, u32[]{:S(2)}, u32[]{:S(2)}) collective-permute-start(bf16[16,112,768]{2,1,0:T(8,128)(2,1)} %constant_dynamic-update-slice_fusion), channel_id=1, source_target_pairs={{0,1},{1,0},{2,3},{3,2},{4,5},{5,4},{6,7},{7,6},{8,9},{9,8},{10,11... | collective-permute-start | bytes 8257544 | tf_op jit(solution)/shard_map/ppermute | solution.py:280
  94.2 19.7 %collective-permute-start.8 = (bf16[8,120,768]{2,1,0:T(8,128)(2,1)}, bf16[8,120,768]{2,1,0:T(8,128)(2,1)}, u32[]{:S(2)}, u32[]{:S(2)}) collective-permute-start(bf16[8,120,768]{2,1,0:T(8,128)(2,1)} %pad_maximum_fusion.7), channel_id=1, source_target_pairs={{0,2},{1,5},{2,0},{3,7},{4,6},{5,1},{6,4},{7,3},{8,10},{9,13},{10,... | collective-permute-start | bytes 4423688 | tf_op jit(solution)/shard_map/ppermute | solution.py:286
  120.7 94.5 %collective-permute-start.9 = (bf16[16,120,768]{2,1,0:T(8,128)(2,1)}, bf16[16,120,768]{2,1,0:T(8,128)(2,1)}, u32[]{:S(2)}, u32[]{:S(2)}) collective-permute-start(bf16[16,120,768]{2,1,0:T(8,128)(2,1)} %constant_dynamic-update-slice_fusion.5), channel_id=1, source_target_pairs={{0,1},{1,0},{2,3},{3,2},{4,5},{5,4},{6,7},{7,6},{8,9},{9,8},{10,11... | collective-permute-start | bytes 8847368 | tf_op jit(solution)/shard_map/ppermute | solution.py:280
  390.6 41.8 %collective-permute-start.27 = (bf16[16,96,768]{2,1,0:T(8,128)(2,1)}, bf16[16,96,768]{2,1,0:T(8,128)(2,1)}, u32[]{:S(2)}, u32[]{:S(2)}) collective-permute-start(bf16[16,96,768]{2,1,0:T(8,128)(2,1)} %broadcast_select_fusion.14), channel_id=1, source_target_pairs={{0,1},{1,0},{2,3},{3,2},{4,5},{5,4},{6,7},{7,6},{8,9},{9,8},{10,11... | collective-permute-start | bytes 7077896 | tf_op jit(solution)/shard_map/ppermute | solution.py:280
  414.6 28.6 %collective-permute-start.15 = (bf16[16,112,768]{2,1,0:T(8,128)(2,1)}, bf16[16,112,768]{2,1,0:T(8,128)(2,1)}, u32[]{:S(2)}, u32[]{:S(2)}) collective-permute-start(bf16[16,112,768]{2,1,0:T(8,128)(2,1)} %broadcast_select_fusion.7), channel_id=1, source_target_pairs={{0,1},{1,0},{2,3},{3,2},{4,5},{5,4},{6,7},{7,6},{8,9},{9,8},{10,11... | collective-permute-start | bytes 8257544 | tf_op jit(solution)/shard_map/ppermute | solution.py:280
  428.0 32.6 %collective-permute-start.21 = (bf16[16,120,768]{2,1,0:T(8,128)(2,1)}, bf16[16,120,768]{2,1,0:T(8,128)(2,1)}, u32[]{:S(2)}, u32[]{:S(2)}) collective-permute-start(bf16[16,120,768]{2,1,0:T(8,128)(2,1)} %broadcast_select_fusion), channel_id=1, source_target_pairs={{0,1},{1,0},{2,3},{3,2},{4,5},{5,4},{6,7},{7,6},{8,9},{9,8},{10,11... | collective-permute-start | bytes 8847368 | tf_op jit(solution)/shard_map/ppermute | solution.py:280
  437.6 16.5 %collective-permute-start.28 = (bf16[8,96,768]{2,1,0:T(8,128)(2,1)}, bf16[8,96,768]{2,1,0:T(8,128)(2,1)}, u32[]{:S(2)}, u32[]{:S(2)}) collective-permute-start(bf16[8,96,768]{2,1,0:T(8,128)(2,1)} %slice.543), channel_id=1, source_target_pairs={{0,2},{1,5},{2,0},{3,7},{4,6},{5,1},{6,4},{7,3},{8,10},{9,13},{10,... | collective-permute-start | bytes 3538952 | tf_op jit(solution)/shard_map/ppermute | solution.py:311
  447.4 27.8 %collective-permute-start.16 = (bf16[8,112,768]{2,1,0:T(8,128)(2,1)}, bf16[8,112,768]{2,1,0:T(8,128)(2,1)}, u32[]{:S(2)}, u32[]{:S(2)}) collective-permute-start(bf16[8,112,768]{2,1,0:T(8,128)(2,1)} %slice.509), channel_id=1, source_target_pairs={{0,2},{1,5},{2,0},{3,7},{4,6},{5,1},{6,4},{7,3},{8,10},{9,13},{10,... | collective-permute-start | bytes 4128776 | tf_op jit(solution)/shard_map/ppermute | solution.py:311
  456.8 16.5 %collective-permute-start.29 = (bf16[4,96,768]{2,1,0:T(8,128)(2,1)}, bf16[4,96,768]{2,1,0:T(8,128)(2,1)S(1)}, u32[]{:S(2)}, u32[]{:S(2)}) collective-permute-start(bf16[4,96,768]{2,1,0:T(8,128)(2,1)} %slice.545), channel_id=1, source_target_pairs={{0,4},{1,3},{2,6},{3,1},{4,0},{5,7},{6,2},{7,5},{8,12},{9,11},{10,... | collective-permute-start | bytes 1769480 | tf_op jit(solution)/shard_map/ppermute | solution.py:311
  464.1 34.2 %collective-permute-start.22 = (bf16[8,120,768]{2,1,0:T(8,128)(2,1)S(1)}, bf16[8,120,768]{2,1,0:T(8,128)(2,1)S(1)}, u32[]{:S(2)}, u32[]{:S(2)}) collective-permute-start(bf16[8,120,768]{2,1,0:T(8,128)(2,1)S(1)} %slice.526), channel_id=1, source_target_pairs={{0,2},{1,5},{2,0},{3,7},{4,6},{5,1},{6,4},{7,3},{8,10},{9,13},{10,... | collective-permute-start | bytes 4423688 | tf_op jit(solution)/shard_map/ppermute | solution.py:311
  473.4 7.4 %collective-permute-start.30 = (bf16[2,96,768]{2,1,0:T(8,128)(2,1)S(1)}, bf16[2,96,768]{2,1,0:T(8,128)(2,1)S(1)}, u32[]{:S(2)}, u32[]{:S(2)}) collective-permute-start(bf16[2,96,768]{2,1,0:T(8,128)(2,1)S(1)} %slice.547), channel_id=1, source_target_pairs={{0,8},{1,9},{2,10},{3,11},{4,12},{5,13},{6,14},{7,15},{8,0},{9,1},... | collective-permute-start | bytes 884744 | tf_op jit(solution)/shard_map/ppermute | solution.py:311
  477.0 18.4 %collective-permute-start.17 = (bf16[4,112,768]{2,1,0:T(8,128)(2,1)S(1)}, bf16[4,112,768]{2,1,0:T(8,128)(2,1)S(1)}, u32[]{:S(2)}, u32[]{:S(2)}) collective-permute-start(bf16[4,112,768]{2,1,0:T(8,128)(2,1)S(1)} %slice.511), channel_id=1, source_target_pairs={{0,4},{1,3},{2,6},{3,1},{4,0},{5,7},{6,2},{7,5},{8,12},{9,11},{10,... | collective-permute-start | bytes 2064392 | tf_op jit(solution)/shard_map/ppermute | solution.py:311
  480.9 7.7 %collective-permute-start.31 = (bf16[1,96,768]{2,1,0:T(8,128)(2,1)S(1)}, bf16[1,96,768]{2,1,0:T(8,128)(2,1)S(1)}, u32[]{:S(2)}, u32[]{:S(2)}) collective-permute-start(bf16[1,96,768]{2,1,0:T(8,128)(2,1)S(1)} %slice.549), channel_id=1, source_target_pairs={{0,16},{1,17},{2,18},{3,19},{4,20},{5,21},{6,22},{7,23},{8,24},{9,... | collective-permute-start | bytes 442376 | tf_op jit(solution)/shard_map/ppermute | solution.py:311
  488.6 11.6 %collective-permute-start.32 = (bf16[96,768]{1,0:T(8,128)(2,1)S(1)}, bf16[96,768]{1,0:T(8,128)(2,1)S(1)}, u32[]{:S(2)}, u32[]{:S(2)}) collective-permute-start(bf16[96,768]{1,0:T(8,128)(2,1)S(1)} %fusion.55), channel_id=1, source_target_pairs={{0,1},{1,0},{2,3},{3,2},{4,5},{5,4},{6,7},{7,6},{8,9},{9,8},{10,11... | collective-permute-start | bytes 442376 | tf_op jit(solution)/shard_map/ppermute | solution.py:280
  495.6 8.0 %collective-permute-start.18 = (bf16[2,112,768]{2,1,0:T(8,128)(2,1)S(1)}, bf16[2,112,768]{2,1,0:T(8,128)(2,1)S(1)}, u32[]{:S(2)}, u32[]{:S(2)}) collective-permute-start(bf16[2,112,768]{2,1,0:T(8,128)(2,1)S(1)} %slice.513), channel_id=1, source_target_pairs={{0,8},{1,9},{2,10},{3,11},{4,12},{5,13},{6,14},{7,15},{8,0},{9,1},... | collective-permute-start | bytes 1032200 | tf_op jit(solution)/shard_map/ppermute | solution.py:311
  498.5 13.5 %collective-permute-start.23 = (bf16[4,120,768]{2,1,0:T(8,128)(2,1)S(1)}, bf16[4,120,768]{2,1,0:T(8,128)(2,1)S(1)}, u32[]{:S(2)}, u32[]{:S(2)}) collective-permute-start(bf16[4,120,768]{2,1,0:T(8,128)(2,1)S(1)} %slice.528), channel_id=1, source_target_pairs={{0,4},{1,3},{2,6},{3,1},{4,0},{5,7},{6,2},{7,5},{8,12},{9,11},{10,... | collective-permute-start | bytes 2211848 | tf_op jit(solution)/shard_map/ppermute | solution.py:311
  503.7 8.2 %collective-permute-start.19 = (bf16[1,112,768]{2,1,0:T(8,128)(2,1)S(1)}, bf16[1,112,768]{2,1,0:T(8,128)(2,1)S(1)}, u32[]{:S(2)}, u32[]{:S(2)}) collective-permute-start(bf16[1,112,768]{2,1,0:T(8,128)(2,1)S(1)} %slice.515), channel_id=1, source_target_pairs={{0,16},{1,17},{2,18},{3,19},{4,20},{5,21},{6,22},{7,23},{8,24},{9,... | collective-permute-start | bytes 516104 | tf_op jit(solution)/shard_map/ppermute | solution.py:311
  512.2 11.0 %collective-permute-start.24 = (bf16[2,120,768]{2,1,0:T(8,128)(2,1)S(1)}, bf16[2,120,768]{2,1,0:T(8,128)(2,1)S(1)}, u32[]{:S(2)}, u32[]{:S(2)}) collective-permute-start(bf16[2,120,768]{2,1,0:T(8,128)(2,1)S(1)} %slice.530), channel_id=1, source_target_pairs={{0,8},{1,9},{2,10},{3,11},{4,12},{5,13},{6,14},{7,15},{8,0},{9,1},... | collective-permute-start | bytes 1105928 | tf_op jit(solution)/shard_map/ppermute | solution.py:311
  523.3 11.2 %collective-permute-start.25 = (bf16[1,120,768]{2,1,0:T(8,128)(2,1)S(1)}, bf16[1,120,768]{2,1,0:T(8,128)(2,1)S(1)}, u32[]{:S(2)}, u32[]{:S(2)}) collective-permute-start(bf16[1,120,768]{2,1,0:T(8,128)(2,1)S(1)} %slice.532), channel_id=1, source_target_pairs={{0,16},{1,17},{2,18},{3,19},{4,20},{5,21},{6,22},{7,23},{8,24},{9,... | collective-permute-start | bytes 552968 | tf_op jit(solution)/shard_map/ppermute | solution.py:311
  534.5 1.5 collective-permute-start.26
  (89 other events, 830.5 us)

commit v2 on v1

--- a/solution.py
+++ b/solution.py
@@ -4,6 +4,8 @@
 import jax
 import jax.numpy as jnp
 from jax import lax
+from jax.experimental import pallas as pl
+from jax.experimental.pallas import tpu as pltpu
 from jax.sharding import PartitionSpec as P
 
 HEADS = 12
@@ -243,16 +245,19 @@
 
 AXES = ("fsdp", "rep")
 ORDERS = ((8, 4, 2, 1), (8, 4, 1, 2))
+LOW = jnp.bfloat16
+WIDE = jnp.float32
+CHUNK = 256
+SLAB = 128
+VMEM_BYTES = 58 * 1024 * 1024
+CORE_AT, LENGTH_AT, PLACE_AT = 32, 33, 34
 
 
 def mask_table(order):
     masks = [0]
     for bit in order:
-        masks = masks + [bit ^ m for m in masks]
+        masks = masks + [bit ^ mask for mask in masks]
     return masks
-
-
-MASKS = tuple(mask_table(order) for order in ORDERS)
 
 
 def inverse(masks):
@@ -262,7 +267,9 @@
     return places
 
 
+MASKS = tuple(mask_table(order) for order in ORDERS)
 PLACES = tuple(inverse(masks) for masks in MASKS)
+CORE_PAIRS = [(chip * 2 + core, chip * 2 + 1 - core) for chip in range(16) for core in range(2)]
 
 
 def step_pairs(step):
@@ -273,47 +280,784 @@
     ]
 
 
-CORE_PAIRS = [(chip * 2 + core, chip * 2 + 1 - core) for chip in range(16) for core in range(2)]
-
-
 def swap_cores(block):
     return lax.ppermute(block, AXES, CORE_PAIRS)
 
 
-def gather_blocks(own_half):
+def gather_mine(own_half):
     held = own_half[None]
     for step in range(4):
         held = jnp.concatenate([held, lax.ppermute(held, AXES, step_pairs(step))], axis=0)
+    return held
+
+
+def gather_blocks(own_half):
+    held = gather_mine(own_half)
     return held, swap_cores(held)
 
 
-def in_order(mine, other):
-    chip, core = lax.axis_index("fsdp"), lax.axis_index("rep")
-    places = jnp.array(PLACES, jnp.int32)
-    blocks = jnp.arange(16) ^ chip
-    mine = jnp.take(mine, places[core][blocks], axis=0)
-    other = jnp.take(other, places[1 - core][blocks], axis=0)
-    first = jnp.where(core == 0, mine, other)
-    second = jnp.where(core == 0, other, mine)
-    return first, second
-
-
-def scatter_blocks(first, second):
-    chip, core = lax.axis_index("fsdp"), lax.axis_index("rep")
-    masks = jnp.array(MASKS, jnp.int32)
-    keep = jnp.where(core == 0, first, second)
-    send = jnp.where(core == 0, second, first)
-    keep = jnp.take(keep, masks[core] ^ chip, axis=0)
-    send = jnp.take(send, masks[1 - core] ^ chip, axis=0)
-    held = keep + swap_cores(send)
+def scatter_mine(held):
     for step in (3, 2, 1, 0):
         half = held.shape[0] // 2
-        held = held[:half] + lax.ppermute(held[half:], AXES, step_pairs(step))
-    mine = held[0]
+        arrived = lax.ppermute(held[half:], AXES, step_pairs(step))
+        held = held[:half] + arrived
+    return held[0]
+
+
+def scatter_blocks(keep, send):
+    core = lax.axis_index("rep")
+    mine = scatter_mine(keep + swap_cores(send))
     other = swap_cores(mine)
     first = jnp.where(core == 0, mine, other)
     second = jnp.where(core == 0, other, mine)
-    return first, second
+    return first.astype(WIDE), second.astype(WIDE)
+
+
+def dot(left_op, right_op, left_dim, right_dim):
+    return lax.dot_general(
+        left_op,
+        right_op,
+        (((left_dim,), (right_dim,)), ((), ())),
+        preferred_element_type=WIDE,
+    )
+
+
+def each(count, size, body):
+    def step(index, carry):
+        body(pl.ds(pl.multiple_of(index * size, size), size))
+        return carry
+
+    lax.fori_loop(0, count // size, step, 0)
+
+
+def block_at(index):
+    return pl.ds(pl.multiple_of(index * 48, 16), 48)
+
+
+def turned(block):
+    return (block & 3) | ((block & 4) << 1) | ((block & 8) >> 1)
+
+
+def run_copies(make, count):
+    def start(place, carry):
+        for copy in make(place):
+            copy.start()
+        return carry
+
+    def wait(place, carry):
+        for copy in make(place):
+            copy.wait()
+        return carry
+
+    lax.fori_loop(0, count, start, 0)
+    lax.fori_loop(0, count, wait, 0)
+
+
+def attn_copies(scal, mine, other, mats, sem, place):
+    core = scal[CORE_AT]
+    copies = []
+    for source, base, half in ((mine, 0, core), (other, 16, 1 - core)):
+        block = scal[base + place]
+        for part in range(2):
+            row = block if part == 0 else jnp.where(half == 1, turned(block), block)
+            copies.append(
+                pltpu.make_async_copy(
+                    source.at[place, pl.ds(48 * part, 48)],
+                    mats.at[2 * half + part, block_at(row)],
+                    sem,
+                )
+            )
+    return copies
+
+
+def head_masks(dtype):
+    lane = lax.broadcasted_iota(jnp.int32, (1, 128), 1)
+    first = jnp.where(lane < 64, 1.0, 0.0)
+    return (first.astype(dtype), (1.0 - first).astype(dtype))
+
+
+def attend_kernel(
+    scal,
+    tokens,
+    vec,
+    sines,
+    cosines,
+    encoded,
+    mine,
+    other,
+    q_out,
+    k_out,
+    v_out,
+    ctx_out,
+    prob_out,
+    mats,
+    right,
+    sem,
+):
+    pair = pl.program_id(0)
+    width = tokens.shape[1]
+    rows = tokens.shape[0]
+
+    @pl.when(pair == 0)
+    def _():
+        run_copies(partial(attn_copies, scal, mine, other, mats, sem), 16)
+        right[:, :width] = encoded[...]
+
+        def project(at):
+            x = tokens[at, :]
+            q_out[at, :] = (dot(x, mats[0], 1, 0) + vec[4:5, :]).astype(LOW)
+            k_out[at, :] = dot(x, mats[1], 1, 0).astype(LOW)
+            v_out[at, :] = (dot(x, mats[2], 1, 0) + vec[5:6, :]).astype(LOW)
+
+        each(rows, CHUNK, project)
+
+    lanes = pl.ds(pl.multiple_of(pair * 128, 128), 128)
+    right[:, width:] = k_out[:, lanes]
+    rel = mats[3, :, lanes]
+    live = lax.broadcasted_iota(jnp.int32, (1, rows), 1) < scal[LENGTH_AT]
+    half = width // 2
+
+    def score(at):
+        q_pair = q_out[at, :] if q_out.shape[1] == 128 else q_out[at, lanes]
+        sin, cos = sines[at, :], cosines[at, :]
+        mixed = []
+        for head, mask in enumerate(head_masks(LOW)):
+            q_head = q_pair * mask
+            table = dot(q_head, rel, 1, 1)
+            us, uc = table[:, :half], table[:, half:]
+            left = jnp.concatenate(
+                [(uc * sin - us * cos).astype(LOW), (us * sin + uc * cos).astype(LOW), q_head], axis=1
+            )
+            s = dot(left, right[...], 1, 1) * HEAD_DIM ** (-0.5)
+            s = jnp.where(live, s, MASK_FILL)
+            top = jnp.max(s, axis=-1, keepdims=True)
+            e = jnp.exp(s - top)
+            prob = e * (1.0 / jnp.sum(e, axis=-1, keepdims=True))
+            prob_out[head, at, :] = prob
+            mixed.append(dot(prob.astype(LOW), v_out[:, lanes], 1, 0))
+        masks = head_masks(WIDE)
+        ctx_out[at, :] = (mixed[0] * masks[0] + mixed[1] * masks[1]).astype(LOW)
+
+    each(rows, CHUNK, score)
+
+
+def any_space():
+    return pl.BlockSpec(memory_space=pl.ANY)
+
+
+def whole(shape):
+    return pl.BlockSpec(shape, lambda *_: (0,) * len(shape))
+
+
+def attend(scal, tokens, vec, sines, cosines, encoded, mine, other):
+    rows, width = tokens.shape
+    cols = mine.shape[2]
+    pairs = cols // 128
+    low = jax.ShapeDtypeStruct((rows, cols), LOW)
+    return pl.pallas_call(
+        attend_kernel,
+        out_shape=(low, low, low, low, jax.ShapeDtypeStruct((2 * pairs, rows, rows), WIDE)),
+        grid_spec=pltpu.PrefetchScalarGridSpec(
+            num_scalar_prefetch=1,
+            grid=(pairs,),
+            in_specs=[
+                whole((rows, width)),
+                whole((vec.shape[0], cols)),
+                whole((rows, width // 2)),
+                whole((rows, width // 2)),
+                whole((rows, width)),
+                any_space(),
+                any_space(),
+            ],
+            out_specs=[whole((rows, cols))] * 3
+            + [
+                pl.BlockSpec((rows, 128), lambda p, _: (0, p)),
+                pl.BlockSpec((2, rows, rows), lambda p, _: (p, 0, 0)),
+            ],
+            scratch_shapes=[
+                pltpu.VMEM((4, width, cols), LOW),
+                pltpu.VMEM((rows, width + 128), LOW),
+                pltpu.SemaphoreType.DMA,
+            ],
+        ),
+        compiler_params=pltpu.CompilerParams(
+            dimension_semantics=("arbitrary",), vmem_limit_bytes=VMEM_BYTES
+        ),
+        cost_estimate=pl.CostEstimate(
+            flops=pairs * 2 * rows * width * 3072, transcendentals=0, bytes_accessed=24 * 1024 * 1024
+        ),
+        name="attend",
+    )(scal, tokens, vec, sines, cosines, encoded, mine, other)
+
+
+CDF_POLY = (
+    -0.020695917308330536,
+    0.09534552693367004,
+    -0.15029412508010864,
+    0.07120334357023239,
+    -0.011180647648870945,
+    0.05997580662369728,
+    0.08762594312429428,
+    0.11413583159446716,
+    0.12694157660007477,
+    0.12694266438484192,
+)
+CDF_SLOPE = 0.45 / math.sqrt(2.0)
+
+
+def gelu_pair(x):
+    size = jnp.abs(x)
+    t = 1.0 / (1.0 + CDF_SLOPE * size)
+    bell = jnp.exp(-0.5 * x * x)
+    poly = CDF_POLY[0]
+    for value in CDF_POLY[1:]:
+        poly = poly * t + value
+    tail = poly * t * bell
+    cdf = jnp.where(x < 0.0, tail, 1.0 - tail)
+    return x * cdf, cdf + x * bell * (1.0 / math.sqrt(2.0 * math.pi))
+
+
+def moments(z):
+    center = z - jnp.mean(z, axis=-1, keepdims=True)
+    r = lax.rsqrt(jnp.mean(center * center, axis=-1, keepdims=True) + EPS_NORM)
+    return center * r, r
+
+
+def norm_back(grad, xh, r, gain):
+    dxh = grad * gain
+    return r * (
+        dxh - jnp.mean(dxh, axis=-1, keepdims=True) - xh * jnp.mean(dxh * xh, axis=-1, keepdims=True)
+    )
+
+
+def total(values):
+    return jnp.sum(values, axis=0, keepdims=True)
+
+
+def two_copies(scal, mine, other, out_mat, up_mat, sem, place):
+    core = scal[CORE_AT]
+    copies = []
+    for source, base, half in ((mine, 0, core), (other, 16, 1 - core)):
+        at = block_at(scal[base + place])
+        copies.append(
+            pltpu.make_async_copy(
+                source.at[place, pl.ds(0, 48)],
+                out_mat.at[at, pl.ds(pl.multiple_of(half * 384, 128), 384)],
+                sem,
+            )
+        )
+        for part in range(4):
+            copies.append(
+                pltpu.make_async_copy(
+                    source.at[place, pl.ds(48 + 48 * part, 48)],
+                    up_mat.at[2 * half + part // 2, at, pl.ds(384 * (part % 2), 384)],
+                    sem,
+                )
+            )
+    return copies
+
+
+def three_copies(scal, mine, other, down_mat, sem, place):
+    core = scal[CORE_AT]
+    return [
+        pltpu.make_async_copy(
+            source.at[place],
+            down_mat.at[pl.ds(pl.multiple_of(scal[base + place] * 192 + half * 96, 32), 96)],
+            sem,
+        )
+        for source, base, half in ((mine, 0, core), (other, 16, 1 - core))
+    ]
+
+
+def route(scal, half, block, source, keep, send, sem, act):
+    core = scal[CORE_AT]
+
+    @pl.when(core == half)
+    def _():
+        act(pltpu.make_async_copy(source, keep(scal[PLACE_AT + block]), sem))
+
+    @pl.when(core != half)
+    def _():
+        act(pltpu.make_async_copy(source, send(scal[PLACE_AT + 16 + block]), sem))
+
+
+def starting(copy):
+    copy.start()
+
+
+def waiting(copy):
+    copy.wait()
+
+
+def feed_kernel(groups, *refs):
+    scal, tokens, cot, vec = refs[:4]
+    ctx_parts = refs[4 : 4 + groups]
+    two_mine, two_other, three_mine, three_other = refs[4 + groups : 8 + groups]
+    (
+        page_out,
+        dh1_out,
+        dctx_out,
+        vec_out,
+        two_keep,
+        two_send,
+        three_keep,
+        three_send,
+        out_mat,
+        up_mat,
+        down_mat,
+        ctx,
+        norm_low,
+        xh1,
+        r1,
+        act,
+        slope,
+        held,
+        df,
+        dpre,
+        dattn,
+        g_out,
+        g_up,
+        g_down,
+        sem_in,
+        sem_up,
+        sem_down,
+        sem_out,
+    ) = refs[8 + groups :]
+    step = pl.program_id(0)
+    rows, width = tokens.shape
+    length = scal[LENGTH_AT]
+
+    @pl.when(step == 0)
+    def _():
+        run_copies(
+            lambda place: two_copies(scal, two_mine, two_other, out_mat, up_mat, sem_in, place)
+            + three_copies(scal, three_mine, three_other, down_mat, sem_in, place),
+            16,
+        )
+        vec_out[...] = jnp.zeros_like(vec_out)
+        cols = width // groups
+        for g in range(groups):
+            ctx[:, cols * g : cols * (g + 1)] = ctx_parts[g][...]
+
+        def first(at):
+            attn = dot(ctx[at, :], out_mat[...], 1, 0) + vec[6:7, :]
+            hat, r = moments(tokens[at, :].astype(WIDE) + attn)
+            normed = hat * vec[0:1, :] + vec[1:2, :]
+            xh1[at, :] = hat
+            r1[at, :] = jnp.broadcast_to(r, (r.shape[0], 128))
+            norm_low[at, :] = normed.astype(LOW)
+            held[at, :] = normed + vec[7:8, :]
+
+        each(rows, CHUNK, first)
+
+    @pl.when(step < 4)
+    def _():
+        def forward(at):
+            pre = dot(norm_low[at, :], up_mat[step], 1, 0) + vec[pl.ds(8 + step, 1), :]
+            value, grad = gelu_pair(pre)
+            low = value.astype(LOW)
+            act[step, at, :] = low
+            slope[step, at, :] = grad
+            held[at, :] += dot(low, down_mat[pl.ds(pl.multiple_of(step * width, width), width), :], 1, 0)
+
+        each(rows, CHUNK, forward)
+
+    @pl.when(step == 3)
+    def _():
+        def second(at):
+            hat, r = moments(held[at, :])
+            place = lax.broadcasted_iota(jnp.int32, (SLAB, 1), 0) + at.start
+            live = jnp.where(place < length, 1.0, 0.0)
+            page_out[at, :] = ((hat * vec[2:3, :] + vec[3:4, :]) * live).astype(LOW)
+            dy = cot[at, :].astype(WIDE) * live
+            vec_out[2:3, :] += total(dy * hat)
+            vec_out[3:4, :] += total(dy)
+            dh2 = norm_back(dy, hat, r, vec[2:3, :])
+            low = dh2.astype(LOW)
+            df[at, :] = low
+            vec_out[7:8, :] += total(low.astype(WIDE))
+            held[at, :] = dh2
+
+        each(rows, SLAB, second)
+
+    def up_route(slot, unit, act_on):
+        def body(block, carry):
+            for part in range(2):
+                local = 2 * lax.rem(unit, 2) + part
+                at = pl.ds(pl.multiple_of(48 + 48 * local, 16), 48)
+                route(
+                    scal,
+                    unit // 2,
+                    block,
+                    g_up.at[slot, block_at(block), pl.ds(384 * part, 384)],
+                    lambda place: two_keep.at[place, at],
+                    lambda place: two_send.at[place, at],
+                    sem_up.at[slot],
+                    act_on,
+                )
+            return carry
+
+        lax.fori_loop(0, 16, body, 0)
+
+    def down_route(slot, unit, act_on):
+        for part in range(8):
+            route(
+                scal,
+                part % 2,
+                4 * unit + part // 2,
+                g_down.at[slot, pl.ds(96 * part, 96)],
+                lambda place: three_keep.at[place],
+                lambda place: three_send.at[place],
+                sem_down.at[slot],
+                act_on,
+            )
+
+    def out_route(act_on):
+        def body(block, carry):
+            for half in range(2):
+                route(
+                    scal,
+                    half,
+                    block,
+                    g_out.at[block_at(block), pl.ds(384 * half, 384)],
+                    lambda place: two_keep.at[place, pl.ds(0, 48)],
+                    lambda place: two_send.at[place, pl.ds(0, 48)],
+                    sem_out,
+                    act_on,
+                )
+            return carry
+
+        lax.fori_loop(0, 16, body, 0)
+
+    @pl.when(step >= 4)
+    def _():
+        unit = step - 4
+        slot = lax.rem(unit, 2)
+        down_at = pl.ds(pl.multiple_of(unit * width, width), width)
+
+        @pl.when(unit >= 2)
+        def _():
+            up_route(slot, unit - 2, waiting)
+            down_route(slot, unit - 2, waiting)
+
+        def backward(at):
+            grad = dot(df[at, :], down_mat[down_at, :], 1, 1) * slope[unit, at, :]
+            low = grad.astype(LOW)
+            dpre[at, :] = low
+            vec_out[pl.ds(8 + unit, 1), :] += total(low.astype(WIDE))
+            held[at, :] += dot(low, up_mat[unit], 1, 1)
+
+        each(rows, CHUNK, backward)
+
+        def weights(at):
+            g_down[slot, at, :] = dot(act[unit, :, at], df[...], 0, 0).astype(LOW)
+            g_up[slot, at, :] = dot(norm_low[:, at], dpre[...], 0, 0).astype(LOW)
+
+        each(width, CHUNK, weights)
+        down_route(slot, unit, starting)
+        up_route(slot, unit, starting)
+
+    @pl.when(step == 7)
+    def _():
+        def last(at):
+            grad, hat = held[at, :], xh1[at, :]
+            vec_out[0:1, :] += total(grad * hat)
+            vec_out[1:2, :] += total(grad)
+            dh1 = norm_back(grad, hat, r1[at, :1], vec[0:1, :])
+            dh1_out[at, :] = dh1
+            low = dh1.astype(LOW)
+            dattn[at, :] = low
+            vec_out[6:7, :] += total(low.astype(WIDE))
+
+        each(rows, SLAB, last)
+
+        def context(at):
+            dctx_out[at, :] = dot(dattn[at, :], out_mat[...], 1, 1).astype(LOW)
+
+        each(rows, CHUNK, context)
+
+        def weights(at):
+            g_out[at, :] = dot(ctx[:, at], dattn[...], 0, 0).astype(LOW)
+
+        each(width, CHUNK, weights)
+        out_route(starting)
+        for unit in (2, 3):
+            up_route(unit % 2, unit, waiting)
+            down_route(unit % 2, unit, waiting)
+        out_route(waiting)
+
+
+def feed(scal, tokens, cot, vec, ctx_parts, two, three):
+    rows, width = tokens.shape
+    groups = len(ctx_parts)
+    return pl.pallas_call(
+        partial(feed_kernel, groups),
+        out_shape=(
+            jax.ShapeDtypeStruct((rows, width), LOW),
+            jax.ShapeDtypeStruct((rows, width), WIDE),
+            jax.ShapeDtypeStruct((rows, width), LOW),
+            jax.ShapeDtypeStruct((16, width), WIDE),
+            jax.ShapeDtypeStruct((16, 240, 384), LOW),
+            jax.ShapeDtypeStruct((16, 240, 384), LOW),
+            jax.ShapeDtypeStruct((16, 96, width), LOW),
+            jax.ShapeDtypeStruct((16, 96, width), LOW),
+        ),
+        grid_spec=pltpu.PrefetchScalarGridSpec(
+            num_scalar_prefetch=1,
+            grid=(8,),
+            in_specs=[whole((rows, width)), whole((rows, width)), whole((16, width))]
+            + [whole((rows, width // groups))] * groups
+            + [any_space()] * 4,
+            out_specs=[whole((rows, width))] * 3 + [whole((16, width))] + [any_space()] * 4,
+            scratch_shapes=[
+                pltpu.VMEM((width, width), LOW),
+                pltpu.VMEM((4, width, width), LOW),
+                pltpu.VMEM((4 * width, width), LOW),
+                pltpu.VMEM((rows, width), LOW),
+                pltpu.VMEM((rows, width), LOW),
+                pltpu.VMEM((rows, width), WIDE),
+                pltpu.VMEM((rows, 128), WIDE),
+                pltpu.VMEM((4, rows, width), LOW),
+                pltpu.VMEM((4, rows, width), WIDE),
+                pltpu.VMEM((rows, width), WIDE),
+                pltpu.VMEM((rows, width), LOW),
+                pltpu.VMEM((rows, width), LOW),
+                pltpu.VMEM((rows, width), LOW),
+                pltpu.VMEM((width, width), LOW),
+                pltpu.VMEM((2, width, width), LOW),
+                pltpu.VMEM((2, width, width), LOW),
+                pltpu.SemaphoreType.DMA,
+                pltpu.SemaphoreType.DMA((2,)),
+                pltpu.SemaphoreType.DMA((2,)),
+                pltpu.SemaphoreType.DMA,
+            ],
+        ),
+        compiler_params=pltpu.CompilerParams(
+            dimension_semantics=("arbitrary",), vmem_limit_bytes=VMEM_BYTES
+        ),
+        cost_estimate=pl.CostEstimate(
+            flops=2 * rows * width * width * 27, transcendentals=0, bytes_accessed=32 * 1024 * 1024
+        ),
+        name="feed",
+    )(scal, tokens, cot, vec, *ctx_parts, *two, *three)
+
+
+def unattend_kernel(
+    scal,
+    tokens,
+    sines,
+    cosines,
+    encoded,
+    q_in,
+    k_in,
+    v_in,
+    dctx_in,
+    prob,
+    mine,
+    other,
+    dq_out,
+    dk_out,
+    dv_out,
+    vec_out,
+    keep,
+    send,
+    mats,
+    right,
+    prob_low,
+    ds_low,
+    du_low,
+    q_heads,
+    d_heads,
+    dq_part,
+    grads,
+    sem,
+    sem_out,
+):
+    pair = pl.program_id(0)
+    rows, width = tokens.shape
+    half = width // 2
+    scale = HEAD_DIM ** (-0.5)
+
+    @pl.when(pair == 0)
+    def _():
+        run_copies(partial(attn_copies, scal, mine, other, mats, sem), 16)
+        right[:, :width] = encoded[...]
+
+    lanes = pl.ds(pl.multiple_of(pair * 128, 128), 128)
+    right[:, width:] = k_in[...]
+    rel = mats[3, :, lanes]
+    low_masks, wide_masks = head_masks(LOW), head_masks(WIDE)
+
+    def score(at):
+        sin, cos = sines[at, :], cosines[at, :]
+        dq = None
+        for head in range(2):
+            spot = pl.ds(pl.multiple_of(head * rows + at.start, at.size), at.size)
+            dctx = dctx_in[at, :] * low_masks[head]
+            d_heads[spot, :] = dctx
+            q_heads[spot, :] = q_in[at, :] * low_masks[head]
+            p = prob[head, at, :]
+            prob_low[spot, :] = p.astype(LOW)
+            dp = dot(dctx, v_in[...], 1, 1)
+            ds = (p * (dp - jnp.sum(p * dp, axis=-1, keepdims=True))).astype(LOW)
+            ds_low[spot, :] = ds
+            dl = dot(ds, right[...], 1, 0) * scale
+            ls, lc = dl[:, :half], dl[:, half:width]
+            du = jnp.concatenate(
+                [(lc * sin - ls * cos).astype(LOW), (ls * sin + lc * cos).astype(LOW)], axis=1
+            )
+            du_low[spot, :] = du
+            part = (dl[:, width:] + dot(du, rel, 1, 0)) * wide_masks[head]
+            dq = part if dq is None else dq + part
+        dq_out[at, lanes] = dq.astype(LOW)
+
+    each(rows, CHUNK, score)
+    dv_out[:, lanes] = dot(prob_low[...], d_heads[...], 0, 0).astype(LOW)
+    dk_out[:, lanes] = (dot(ds_low[...], q_heads[...], 0, 0) * scale).astype(LOW)
+    grads[3, :, lanes] = dot(du_low[...], q_heads[...], 0, 0).astype(LOW)
+
+    @pl.when(pair == pl.num_programs(0) - 1)
+    def _():
+        def weights(at):
+            x = tokens[:, at]
+            grads[0, at, :] = dot(x, dq_out[...], 0, 0).astype(LOW)
+            grads[1, at, :] = dot(x, dk_out[...], 0, 0).astype(LOW)
+            grads[2, at, :] = dot(x, dv_out[...], 0, 0).astype(LOW)
+
+        each(width, CHUNK, weights)
+
+        def move(act_on):
+            def body(block, carry):
+                for slot in range(4):
+                    row = turned(block) if slot == 3 else block
+                    at = pl.ds(48 * (slot % 2), 48)
+                    route(
+                        scal,
+                        slot // 2,
+                        block,
+                        grads.at[slot, block_at(row)],
+                        lambda place: keep.at[place, at],
+                        lambda place: send.at[place, at],
+                        sem_out,
+                        act_on,
+                    )
+                return carry
+
+            lax.fori_loop(0, 16, body, 0)
+
+        move(starting)
+        vec_out[...] = jnp.zeros_like(vec_out)
+        vec_out[0:1, :] = total(dq_out[...].astype(WIDE))
+        vec_out[1:2, :] = total(dv_out[...].astype(WIDE))
+        move(waiting)
+
+
+def unattend(scal, tokens, sines, cosines, encoded, q, k, v, dctx, group, prob, mine, other):
+    rows, width = tokens.shape
+    cols = mine.shape[2]
+    pairs = cols // 128
+    low = jax.ShapeDtypeStruct((rows, cols), LOW)
+    lane_block = pl.BlockSpec((rows, 128), lambda p, _: (0, p))
+    return pl.pallas_call(
+        unattend_kernel,
+        out_shape=(low, low, low, jax.ShapeDtypeStruct((8, cols), WIDE))
+        + (jax.ShapeDtypeStruct((16, 96, cols), LOW),) * 2,
+        grid_spec=pltpu.PrefetchScalarGridSpec(
+            num_scalar_prefetch=1,
+            grid=(pairs,),
+            in_specs=[
+                whole((rows, width)),
+                whole((rows, half_of(width))),
+                whole((rows, half_of(width))),
+                whole((rows, width)),
+                lane_block,
+                lane_block,
+                lane_block,
+                pl.BlockSpec((rows, 128), lambda p, _: (0, group * pairs + p)),
+                pl.BlockSpec((2, rows, rows), lambda p, _: (p, 0, 0)),
+                any_space(),
+                any_space(),
+            ],
+            out_specs=[whole((rows, cols))] * 3 + [whole((8, cols))] + [any_space()] * 2,
+            scratch_shapes=[
+                pltpu.VMEM((4, width, cols), LOW),
+                pltpu.VMEM((rows, width + 128), LOW),
+                pltpu.VMEM((2 * rows, rows), LOW),
+                pltpu.VMEM((2 * rows, rows), LOW),
+                pltpu.VMEM((2 * rows, width), LOW),
+                pltpu.VMEM((2 * rows, 128), LOW),
+                pltpu.VMEM((2 * rows, 128), LOW),
+                pltpu.VMEM((8, 128), WIDE),
+                pltpu.VMEM((4, width, cols), LOW),
+                pltpu.SemaphoreType.DMA,
+                pltpu.SemaphoreType.DMA,
+            ],
+        ),
+        compiler_params=pltpu.CompilerParams(
+            dimension_semantics=("arbitrary",), vmem_limit_bytes=VMEM_BYTES
+        ),
+        cost_estimate=pl.CostEstimate(
+            flops=pairs * 2 * rows * width * 5000, transcendentals=0, bytes_accessed=24 * 1024 * 1024
+        ),
+        name="unattend",
+    )(scal, tokens, sines, cosines, encoded, q, k, v, dctx, prob, mine, other)
+
+
+def half_of(width):
+    return width // 2
+
+
+def input_grad_kernel(groups, *refs):
+    scal, dh1 = refs[:2]
+    parts = refs[2 : 2 + 3 * groups]
+    pieces = refs[2 + 3 * groups : 2 + 5 * groups]
+    out, mats, sem = refs[2 + 5 * groups :]
+
+    def copies(place):
+        made = []
+        for g in range(groups):
+            made += attn_copies(scal, pieces[2 * g], pieces[2 * g + 1], mats.at[g], sem, place)
+        return made
+
+    run_copies(copies, 16)
+
+    def rows_of(at):
+        grad = dh1[at, :]
+        for g in range(groups):
+            for slot in range(3):
+                grad = grad + dot(parts[3 * g + slot][at, :], mats[g, slot], 1, 1)
+        out[at, :] = grad
+
+    each(dh1.shape[0], CHUNK, rows_of)
+
+
+def input_grad(scal, dh1, parts, pieces):
+    rows, width = dh1.shape
+    groups = len(pieces) // 2
+    cols = width // groups
+    return pl.pallas_call(
+        partial(input_grad_kernel, groups),
+        out_shape=jax.ShapeDtypeStruct((rows, width), WIDE),
+        grid_spec=pltpu.PrefetchScalarGridSpec(
+            num_scalar_prefetch=1,
+            grid=(1,),
+            in_specs=[whole((rows, width))]
+            + [whole((rows, cols))] * (3 * groups)
+            + [any_space()] * (2 * groups),
+            out_specs=whole((rows, width)),
+            scratch_shapes=[pltpu.VMEM((groups, 4, width, cols), LOW), pltpu.SemaphoreType.DMA],
+        ),
+        compiler_params=pltpu.CompilerParams(
+            dimension_semantics=("arbitrary",), vmem_limit_bytes=VMEM_BYTES
+        ),
+        cost_estimate=pl.CostEstimate(
+            flops=2 * rows * width * width * 3, transcendentals=0, bytes_accessed=10 * 1024 * 1024
+        ),
+        name="input_grad",
+    )(scal, dh1, *parts, *pieces)
+
+
+GROUPS = 1
 
 
 def local(
@@ -334,64 +1078,109 @@
     down_second,
     vector_second,
 ):
-    core = lax.axis_index("rep")
-    attn_low = attn_weight.astype(jnp.bfloat16)
-    up_low = up_weight.astype(jnp.bfloat16).reshape(48, 4, 768).transpose(1, 0, 2)
-    down_low = down_weight.astype(jnp.bfloat16).reshape(4, 48, 768)
-    vec_low = jnp.pad(vectors.astype(jnp.bfloat16), ((0, 4), (0, 768 - 48)))
-    halves_one = jnp.stack([
-        jnp.concatenate([attn_low[0], attn_low[1], vec_low]),
-        jnp.concatenate([attn_low[2], attn_low[4], vec_low]),
-    ])
-    halves_two = jnp.stack([
-        jnp.concatenate([attn_low[3, :, :384].reshape(24, 768), up_low[0], up_low[1]]),
-        jnp.concatenate([attn_low[3, :, 384:].reshape(24, 768), up_low[2], up_low[3]]),
-    ])
-    halves_three = jnp.stack([
-        jnp.concatenate([down_low[0], down_low[1]]),
-        jnp.concatenate([down_low[2], down_low[3]]),
-    ])
-    def own(halves):
-        return lax.dynamic_index_in_dim(halves, core, 0, keepdims=False)
-    one = in_order(*gather_blocks(own(halves_one)))
-    two = in_order(*gather_blocks(own(halves_two)))
-    three = in_order(*gather_blocks(own(halves_three)))
-    def square(piece, start):
-        return piece[:, start:start + 48].reshape(768, 768)
-    w_o = jnp.concatenate([p[:, :24].reshape(768, 384) for p in two], axis=1)
-    attn_full = jnp.stack([square(one[0], 0), square(one[0], 48), square(one[1], 0), w_o, square(one[1], 48)])
-    up_full = jnp.concatenate([square(p, 24 + 48 * i) for p in two for i in range(2)], axis=1)
-    down_full = jnp.concatenate(three, axis=1).reshape(3072, 768)
-    vec_full = one[0][:, 96:108, :48].transpose(1, 0, 2).reshape(12, 768)
-    weights = (attn_full, up_full, down_full, vec_full)
-    page_out, saved_state = forward_page(weights, tokens[0], boxes[0], lengths[0])
-    layer_out = page_out[None]
-    token_grad, (attn_grads, up_grad, down_grad, vector_grad) = backward_page(
-        weights, tokens[0], boxes[0], lengths[0], cotangent[0], saved_state
-    )
-    token_grad = token_grad[None]
-    def low(v):
-        return v.astype(jnp.bfloat16)
-    down_blocks = low(down_grad).reshape(16, 192, 768)
-    three = scatter_blocks(down_blocks[:, :96], down_blocks[:, 96:])
-    up_blocks = low(up_grad).reshape(16, 48, 4, 768).transpose(0, 2, 1, 3)
-    attn_blocks = low(attn_grads).reshape(5, 16, 48, 768)
-    o_blocks = attn_blocks[3]
-    two = scatter_blocks(
-        *(jnp.concatenate([o_blocks[:, :, 384 * i:384 * i + 384].reshape(16, 24, 768), up_blocks[:, 2 * i], up_blocks[:, 2 * i + 1]], axis=1)
-        for i in range(2)))
-    vec_blocks = jnp.pad(low(vector_grad).reshape(12, 16, 48).transpose(1, 0, 2), ((0, 0), (0, 4), (0, 720)))
-    one = scatter_blocks(
-        jnp.concatenate([attn_blocks[0], attn_blocks[1], vec_blocks], axis=1),
-        jnp.concatenate([attn_blocks[2], attn_blocks[4], vec_blocks], axis=1))
-    wide = [v.astype(jnp.float32) for v in (*one, *two, *three)]
-    o_sum = jnp.concatenate([wide[2][:24].reshape(48, 384), wide[3][:24].reshape(48, 384)], axis=1)
+    chip, core = lax.axis_index("fsdp"), lax.axis_index("rep")
+    width = tokens.shape[2]
+    cols = width // GROUPS
+    masks, places = jnp.array(MASKS, jnp.int32), jnp.array(PLACES, jnp.int32)
+    lane = jnp.arange(16, dtype=jnp.int32)
+    scal = jnp.concatenate(
+        [
+            masks[core] ^ chip,
+            masks[1 - core] ^ chip,
+            jnp.stack([core, lengths[0]]),
+            places[core][lane ^ chip],
+            places[1 - core][lane ^ chip],
+        ]
+    ).astype(jnp.int32)
+
+    first = core == 0
+    top = jnp.where(first, attn_weight[0], attn_weight[2]).astype(LOW)
+    bottom = jnp.where(first, attn_weight[1], attn_weight[4]).astype(LOW)
+    own_one = jnp.concatenate([top, bottom], axis=0)
+    one = [
+        gather_blocks(own_one[:, cols * g : cols * (g + 1)]) for g in range(GROUPS)
+    ]
+    vec_blocks = gather_mine(vectors.astype(LOW))
+    vec = jnp.take(vec_blocks, places[core][lane ^ chip], axis=0)
+    vec = vec.transpose(1, 0, 2).reshape(vectors.shape[0], width).astype(WIDE)
+    vec = jnp.pad(vec, ((0, 16 - vec.shape[0]), (0, 0)))
+    parts = [attn_weight[3]] + [up_weight[:, 768 * i : 768 * (i + 1)] for i in range(4)]
+    halves = [
+        [parts[0][:, 384 * h : 384 * (h + 1)]]
+        + [up_weight[:, 1536 * h + 384 * i : 1536 * h + 384 * (i + 1)] for i in range(4)]
+        for h in range(2)
+    ]
+    own_two = jnp.concatenate(
+        [jnp.where(first, a, b).astype(LOW) for a, b in zip(*halves, strict=True)], axis=0
+    )
+    two = gather_blocks(own_two)
+    own_three = jnp.where(first, down_weight[:96], down_weight[96:]).astype(LOW)
+    three = gather_blocks(own_three)
+
+    quarter = width // 4
+    frequency = jnp.exp(jnp.arange(quarter).astype(WIDE) * (-math.log(10000.0) / quarter))
+    place = boxes[0].astype(WIDE)
+    angles = jnp.concatenate([place[0][:, None] * frequency, place[1][:, None] * frequency], axis=1)
+    sines, cosines = jnp.sin(angles), jnp.cos(angles)
+    encoded = jnp.concatenate([sines, cosines], axis=1).astype(LOW)
+
+    page = tokens[0]
+    kept = []
+    for g in range(GROUPS):
+        vec_group = vec[:, cols * g : cols * (g + 1)]
+        kept.append(attend(scal, page, vec_group, sines, cosines, encoded, *one[g]))
+    page_out, dh1, dctx, vec_one, two_keep, two_send, three_keep, three_send = feed(
+        scal, page, cotangent[0], vec, [k[3] for k in kept], two, three
+    )
+    three_sum = scatter_blocks(three_keep, three_send)
+    two_sum = scatter_blocks(two_keep, two_send)
+    back = [
+        unattend(
+            scal,
+            page,
+            sines,
+            cosines,
+            encoded,
+            *kept[g][:3],
+            dctx,
+            g,
+            kept[g][4],
+            *one[g],
+        )
+        for g in range(GROUPS)
+    ]
+    one_sum = [scatter_blocks(b[4], b[5]) for b in back]
+    vec_two = jnp.concatenate([b[3][:2] for b in back], axis=1)
+    vec_grad = jnp.concatenate([vec_one[:4], vec_two, vec_one[6:12]], axis=0)
+    vec_blocks = vec_grad.reshape(12, 16, 48).transpose(1, 0, 2)
+    vec_blocks = jnp.take(vec_blocks, masks[core] ^ chip, axis=0)
+    vec_mine = scatter_mine(vec_blocks)
+    vec_other = swap_cores(vec_mine)
+    vec_sum = vec_mine + vec_other
+    token_grad = input_grad(
+        scal,
+        dh1,
+        [part for b in back for part in b[:3]],
+        [piece for pieces in one for piece in pieces],
+    )
+    halves_one = [jnp.concatenate([s[h] for s in one_sum], axis=1) for h in range(2)]
     reduced = (
-        jnp.stack([wide[0][:48], wide[0][48:96], wide[1][:48], o_sum, wide[1][48:96]]),
-        jnp.concatenate([wide[2][24:72], wide[2][72:], wide[3][24:72], wide[3][72:]], axis=1),
-        jnp.concatenate([wide[4], wide[5]], axis=0),
-        wide[0][96:108, :48],
-    )
+        jnp.stack(
+            [
+                halves_one[0][:48],
+                halves_one[0][48:],
+                halves_one[1][:48],
+                jnp.concatenate([two_sum[0][:48], two_sum[1][:48]], axis=1),
+                halves_one[1][48:],
+            ]
+        ),
+        jnp.concatenate(
+            [two_sum[h][48 + 48 * i : 96 + 48 * i] for h in range(2) for i in range(4)], axis=1
+        ),
+        jnp.concatenate(three_sum, axis=0),
+        vec_sum,
+    )
+    layer_out, token_grad = page_out[None], token_grad[None]
     attn_rates = jnp.array(ATTN_RATES, jnp.float32)[:, None, None]
     attn_new, attn_first_new, attn_second_new = adam_update(
         attn_weight, attn_first, attn_second, reduced[0], attn_rates, WEIGHT_DECAY

time: 555 us -> 359 us (0.65); the launches traced: 545 us -> 358 us
  matrix products: 144 us -> 0 us
  Pallas kernels: 0 us -> 127 us
  local copies, waits for them, and re-layouts: 133 us -> 28.4 us
  other arithmetic: 123 us -> 37.6 us
  waiting for transfers between devices: 107 us -> 118 us
  starting transfers between devices: 34.6 us -> 43.7 us
    dot_general x23 -> x0, matrix products: 144 us -> none  [the longest x6 26.2 us: contract(): lax.dot_general(left_op, right_op, (((left_dim,), (right_dim,)), ((), ())...]
    pallas_call x0 -> x4, Pallas kernels: none -> 127 us  [the longest x1 46.7 us: feed(): pl.pallas_call(partial(feed_kernel, groups), out_shape=(jax.ShapeDtypeStr...]
    gather x14 -> x4, local copies, waits for them, and re-layouts: 43.3 us -> 4 us  [the longest x1 2.11 us: local(): vec_blocks = jnp.take(vec_blocks, masks[core] ^ chip, axis=0)]
    select_n x12 -> x4, other arithmetic: 29 us -> 0.1 us  [the longest x2 0.09 us: local(): vec_blocks = jnp.take(vec_blocks, masks[core] ^ chip, axis=0)]
    another operation x5 -> x1, other arithmetic: 30.6 us -> 3.86 us
    another operation x13 -> x1, local copies, waits for them, and re-layouts: 17.3 us -> 0.01 us  [local(): jnp.stack([halves_one[0][:48], halves_one[0][48:], halves_one[1][:48], jn...]
    reshape x9 -> x2, local copies, waits for them, and re-layouts: 18.5 us -> 3.11 us  [local(): vec_blocks = vec_grad.reshape(12, 16, 48).transpose(1, 0, 2)]
    slice x32 -> x20, local copies, waits for them, and re-layouts: 17.7 us -> 4.6 us  [the longest x16 3.85 us: scatter_mine(): arrived = lax.ppermute(held[half:], AXES, step_pairs(step))]
  transfers between devices with their start and end apart: 33 -> 42, of which waited for: 22 -> 23; matrix products, arithmetic and copies ran while one was open for 38% -> 17% of each run, Pallas kernels for 0% -> 12%
where the time goes in v2:
time: 359 us; the launch traced here: 358 us
  Pallas kernels  127 us (35%)
  waiting for transfers between devices  118 us (33%)
  starting transfers between devices  43.7 us (12%)
  other arithmetic  37.6 us (10%)
  local copies, waits for them, and re-layouts  28.4 us (8%)
    ppermute x16, waiting for transfers between devices, gather_mine(): lax.ppermute(held, AXES, step_pairs(step))  54.6 us
    ppermute x16, waiting for transfers between devices, scatter_mine(): arrived = lax.ppermute(held[half:], AXES, step_pairs(step))  54.6 us
    pallas_call x1, Pallas kernels, feed(): pl.pallas_call(partial(feed_kernel, groups), out_shape=(jax.ShapeDtypeStr...  46.7 us
    pallas_call x1, Pallas kernels, unattend(): pl.pallas_call(unattend_kernel, out_shape=(low, low, low, jax.ShapeDtypeS...  39.5 us
    pallas_call x1, Pallas kernels, attend(): pl.pallas_call(attend_kernel, out_shape=(low, low, low, low, jax.ShapeDty...  32.3 us
    ppermute x16, starting transfers between devices, scatter_mine(): arrived = lax.ppermute(held[half:], AXES, step_pairs(step))  22.6 us
    ppermute x16, starting transfers between devices, gather_mine(): lax.ppermute(held, AXES, step_pairs(step))  19.5 us
    unnamed x63, local copies, waits for them, and re-layouts  9.64 us
  transfers between devices with their start and end apart: 42, of which 23 were waited for; matrix products, arithmetic and copies ran while one was open for 17% of the time, Pallas kernels for 12%

profile of v2, /device:TPU:0, one launch (start us, length us, event | category | flops | bytes accessed | tf_op | source)
XLA Modules:
  0.0 357.6 jit_solution(5170061776106420582)
XLA Ops:
  1.4 4.0 %collective-permute-start = (bf16[1,12,48]{2,1,0:T(8,128)(2,1)S(1)}, bf16[1,12,48]{2,1,0:T(8,128)(2,1)S(1)}, u32[]{:S(2)}, u32[]{:S(2)}) collective-permute-start(bf16[1,12,48]{2,1,0:T(8,128)(2,1)S(1)} %get-tuple-element.79), channel_id=1, source_target_pairs={{0,16},{1,17},{2,18},{3,19},{4,20},{5,21},{6,22},{7,23},{8,24},{9,... | collective-permute-start | bytes 3464 | tf_op jit(solution)/shard_map/ppermute | solution.py:290
  10.5 3.0 collective-permute-start.9
  17.2 7.3 %collective-permute-done.4 = bf16[1,96,768]{2,1,0:T(8,128)(2,1)S(1)} collective-permute-done((bf16[1,96,768]{2,1,0:T(8,128)(2,1)S(1)}, bf16[1,96,768]{2,1,0:T(8,128)(2,1)S(1)}, u32[]{:S(2)}, u32[]{:S(2)}) %collective-permute-start.4) | collective-permute-done | bytes 147488 | tf_op jit(solution)/shard_map/ppermute | solution.py:290
  24.6 3.8 %collective-permute-done.9 = bf16[1,240,384]{2,1,0:T(8,128)(2,1)S(1)} collective-permute-done((bf16[1,240,384]{2,1,0:T(8,128)(2,1)S(1)}, bf16[1,240,384]{2,1,0:T(8,128)(2,1)S(1)}, u32[]{:S(2)}, u32[]{:S(2)}) %collective-permute-start.9) | collective-permute-done | bytes 184352 | tf_op jit(solution)/shard_map/ppermute | solution.py:290
  29.3 7.5 %collective-permute-done.5 = bf16[2,96,768]{2,1,0:T(8,128)(2,1)S(1)} collective-permute-done((bf16[2,96,768]{2,1,0:T(8,128)(2,1)S(1)}, bf16[2,96,768]{2,1,0:T(8,128)(2,1)S(1)}, u32[]{:S(2)}, u32[]{:S(2)}) %collective-permute-start.5) | collective-permute-done | bytes 294944 | tf_op jit(solution)/shard_map/ppermute | solution.py:290
  38.4 6.0 %collective-permute-done.10 = bf16[2,240,384]{2,1,0:T(8,128)(2,1)S(1)} collective-permute-done((bf16[2,240,384]{2,1,0:T(8,128)(2,1)S(1)}, bf16[2,240,384]{2,1,0:T(8,128)(2,1)S(1)}, u32[]{:S(2)}, u32[]{:S(2)}) %collective-permute-start.10) | collective-permute-done | bytes 368672 | tf_op jit(solution)/shard_map/ppermute | solution.py:290
  46.0 3.9 %fusion.39 = (bf16[512,384]{1,0:T(8,128)(2,1)S(1)}, f32[512,384]{1,0:T(8,128)}, bf16[512,384]{1,0:T(8,128)(2,1)S(1)}, f32[512,384]{1,0:T(8,128)}) fusion(f32[512,192]{1,0:T(8,128)S(1)} %copy-done.2, f32[512,192]{1,0:T(8,128)S(1)} %copy-done.1), kind=kLoop, calls=%fused_computation.157 | loop fusion | flops 589824 | bytes 3145728 | tf_op jit(solution)/shard_map/convert.6
  54.3 4.1 %collective-permute-done.15 = bf16[2,96,768]{2,1,0:T(8,128)(2,1)S(1)} collective-permute-done((bf16[2,96,768]{2,1,0:T(8,128)(2,1)S(1)}, bf16[2,96,768]{2,1,0:T(8,128)(2,1)S(1)}, u32[]{:S(2)}, u32[]{:S(2)}) %collective-permute-start.15) | collective-permute-done | bytes 294944 | tf_op jit(solution)/shard_map/ppermute | solution.py:290
  66.7 9.2 %collective-permute-done.16 = bf16[4,96,768]{2,1,0:T(8,128)(2,1)} collective-permute-done((bf16[4,96,768]{2,1,0:T(8,128)(2,1)}, bf16[4,96,768]{2,1,0:T(8,128)(2,1)}, u32[]{:S(2)}, u32[]{:S(2)}) %collective-permute-start.16) | collective-permute-done | bytes 589856 | tf_op jit(solution)/shard_map/ppermute | solution.py:290
  78.5 2.3 constant_dynamic-update-slice_fusion.5.mine.refs_5_
  83.3 7.5 %collective-permute-done.12 = bf16[8,240,384]{2,1,0:T(8,128)(2,1)} collective-permute-done((bf16[8,240,384]{2,1,0:T(8,128)(2,1)}, bf16[8,240,384]{2,1,0:T(8,128)(2,1)}, u32[]{:S(2)}, u32[]{:S(2)}) %collective-permute-start.12) | collective-permute-done | bytes 1474592 | tf_op jit(solution)/shard_map/ppermute | solution.py:290
  90.8 2.7 constant_dynamic-update-slice_fusion.15.refs_5_
  98.9 4.4 %collective-permute-done.17 = bf16[8,96,768]{2,1,0:T(8,128)(2,1)S(1)} collective-permute-done((bf16[8,96,768]{2,1,0:T(8,128)(2,1)S(1)}, bf16[8,96,768]{2,1,0:T(8,128)(2,1)S(1)}, u32[]{:S(2)}, u32[]{:S(2)}) %collective-permute-start.17) | collective-permute-done | bytes 1179680 | tf_op jit(solution)/shard_map/ppermute | solution.py:290
  106.0 2.4 collective-permute-done.2
  110.0 2.4 collective-permute-done.3
  113.8 32.3 %attend.1 = (bf16[512,768]{1,0:T(8,128)(2,1)}, bf16[512,768]{1,0:T(8,128)(2,1)}, bf16[512,768]{1,0:T(8,128)(2,1)}, bf16[512,768]{1,0:T(8,128)(2,1)}, f32[12,512,512]{2,1,0:T(8,128)}) custom-call(s32[66]{0:T(128)} %concatenate.91.scal.refs_0_, bf16[512,768]{1,0:T(8,128)(2,1)} %bitcast.86, f32[16,768]{1,0:T(8,128)} %pad_convert_fusion.vec.refs_3_, ...), custom_call_target="tpu_custom_call" | custom-call | flops 14495514624 | bytes 25165824 | tf_op jit(solution)/shard_map/attend/pallas_call | solution.py:457
  146.1 46.7 %feed.1 = (bf16[512,768]{1,0:T(8,128)(2,1)}, f32[512,768]{1,0:T(8,128)}, bf16[512,768]{1,0:T(8,128)(2,1)}, f32[16,768]{1,0:T(8,128)}, bf16[16,240,384]{2,1,0:T(8...) custom-call(s32[66]{0:T(128)} %concatenate.91.scal.refs_0_, ...), custom_call_target="tpu_custom_call" | custom-call | flops 16307453952 | bytes 33554432 | tf_op jit(solution)/shard_map/feed/pallas_call | solution.py:793
  192.9 39.5 %unattend.1 = (bf16[512,768]{1,0:T(8,128)(2,1)}, bf16[512,768]{1,0:T(8,128)(2,1)}, bf16[512,768]{1,0:T(8,128)(2,1)}, f32[8,768]{1,0:T(8,128)}, bf16[16,96,768]{2...) custom-call(s32[66]{0:T(128)} %concatenate.91.scal.refs_0_, bf16[512,768]{1,0:T(8,128)(2,1)} %bitcast.88, ...), custom_call_target="tpu_custom_call" | custom-call | flops 23592960000 | bytes 25165824 | tf_op jit(solution)/shard_map/unattend/pallas_call | solution.py:961
  233.0 6.7 %collective-permute-done.19 = bf16[16,96,768]{2,1,0:T(8,128)(2,1)S(1)} collective-permute-done((bf16[16,96,768]{2,1,0:T(8,128)(2,1)}, bf16[16,96,768]{2,1,0:T(8,128)(2,1)S(1)}, u32[]{:S(2)}, u32[]{:S(2)}) %collective-permute-start.19) | collective-permute-done | bytes 2359328 | tf_op jit(solution)/shard_map/ppermute | solution.py:284
  239.7 2.3 add.180
  251.3 3.1 add.200
  256.8 16.2 %collective-permute-done.37 = f32[8,12,48]{2,1,0:T(8,128)S(1)} collective-permute-done((f32[8,12,48]{2,1,0:T(8,128)S(1)}, f32[8,12,48]{2,1,0:T(8,128)S(1)}, u32[]{:S(2)}, u32[]{:S(2)}) %collective-permute-start.37) | collective-permute-done | bytes 18464 | tf_op jit(solution)/shard_map/ppermute | solution.py:302
  274.4 2.6 collective-permute-done.38
  285.4 9.0 %input_grad.1 = f32[512,768]{1,0:T(8,128)} custom-call(s32[66]{0:T(128)} %concatenate.91.scal.refs_0_, f32[512,768]{1,0:T(8,128)} %get-tuple-element.39.refs_1_, bf16[512,768]{1,0:T(8,128)(2,1)} %get-tuple-element.45.refs_2_, bf16[512,768]{1,0:T(8,128)(2,1)} %get-tuple-element.46.refs_3_, bf16[512,768]{1,0:T(8,128)(2,1)} %get-tuple-element.47.refs_4_, ...), custom_call_target="tpu_custom_call" | custom-call | flops 1811939328 | bytes 10485760 | tf_op jit(solution)/shard_map/input_grad/pallas_call | solution.py:1038
  294.4 2.6 add.185
  305.1 4.4 %collective-permute-done.22 = bf16[2,96,768]{2,1,0:T(8,128)(2,1)S(1)} collective-permute-done((bf16[2,96,768]{2,1,0:T(8,128)(2,1)S(1)}, bf16[2,96,768]{2,1,0:T(8,128)(2,1)S(1)}, u32[]{:S(2)}, u32[]{:S(2)}) %collective-permute-start.22) | collective-permute-done | bytes 294944 | tf_op jit(solution)/shard_map/ppermute | solution.py:302
  309.6 3.0 collective-permute-start.23
  312.6 6.1 %collective-permute-done.34 = bf16[2,96,768]{2,1,0:T(8,128)(2,1)S(1)} collective-permute-done((bf16[2,96,768]{2,1,0:T(8,128)(2,1)S(1)}, bf16[2,96,768]{2,1,0:T(8,128)(2,1)S(1)}, u32[]{:S(2)}, u32[]{:S(2)}) %collective-permute-start.34) | collective-permute-done | bytes 294944 | tf_op jit(solution)/shard_map/ppermute | solution.py:302
  321.1 7.3 %collective-permute-done.35 = bf16[1,96,768]{2,1,0:T(8,128)(2,1)S(1)} collective-permute-done((bf16[1,96,768]{2,1,0:T(8,128)(2,1)S(1)}, bf16[1,96,768]{2,1,0:T(8,128)(2,1)S(1)}, u32[]{:S(2)}, u32[]{:S(2)}) %collective-permute-start.35) | collective-permute-done | bytes 147488 | tf_op jit(solution)/shard_map/ppermute | solution.py:302
  332.3 2.5 collective-permute-start.28
  336.4 5.7 %collective-permute-done.28 = bf16[2,240,384]{2,1,0:T(8,128)(2,1)S(1)} collective-permute-done((bf16[2,240,384]{2,1,0:T(8,128)(2,1)S(1)}, bf16[2,240,384]{2,1,0:T(8,128)(2,1)S(1)}, u32[]{:S(2)}, u32[]{:S(2)}) %collective-permute-start.28) | collective-permute-done | bytes 368672 | tf_op jit(solution)/shard_map/ppermute | solution.py:302
  343.1 8.5 %collective-permute-done.29 = bf16[1,240,384]{2,1,0:T(8,128)(2,1)S(1)} collective-permute-done((bf16[1,240,384]{2,1,0:T(8,128)(2,1)S(1)}, bf16[1,240,384]{2,1,0:T(8,128)(2,1)S(1)}, u32[]{:S(2)}, u32[]{:S(2)}) %collective-permute-start.29) | collective-permute-done | bytes 184352 | tf_op jit(solution)/shard_map/ppermute | solution.py:302
  (220 shorter events, 86.4 us)
Async XLA Ops:
  1.4 92.2 %collective-permute-start = (bf16[1,12,48]{2,1,0:T(8,128)(2,1)S(1)}, bf16[1,12,48]{2,1,0:T(8,128)(2,1)S(1)}, u32[]{:S(2)}, u32[]{:S(2)}) collective-permute-start(bf16[1,12,48]{2,1,0:T(8,128)(2,1)S(1)} %get-tuple-element.79), channel_id=1, source_target_pairs={{0,16},{1,17},{2,18},{3,19},{4,20},{5,21},{6,22},{7,23},{8,24},{9,... | collective-permute-start | bytes 3464 | tf_op jit(solution)/shard_map/ppermute | solution.py:290
  6.7 17.8 %collective-permute-start.4 = (bf16[1,96,768]{2,1,0:T(8,128)(2,1)S(1)}, bf16[1,96,768]{2,1,0:T(8,128)(2,1)S(1)}, u32[]{:S(2)}, u32[]{:S(2)}) collective-permute-start(bf16[1,96,768]{2,1,0:T(8,128)(2,1)S(1)} %maximum_bitcast_fusion), channel_id=1, source_target_pairs={{0,16},{1,17},{2,18},{3,19},{4,20},{5,21},{6,22},{7,23},{8,24},{9,... | collective-permute-start | bytes 442376 | tf_op jit(solution)/shard_map/ppermute | solution.py:290
  10.5 17.9 %collective-permute-start.9 = (bf16[1,240,384]{2,1,0:T(8,128)(2,1)S(1)}, bf16[1,240,384]{2,1,0:T(8,128)(2,1)S(1)}, u32[]{:S(2)}, u32[]{:S(2)}) collective-permute-start(bf16[1,240,384]{2,1,0:T(8,128)(2,1)S(1)} %bitcast.77), channel_id=1, source_target_pairs={{0,16},{1,17},{2,18},{3,19},{4,20},{5,21},{6,22},{7,23},{8,24},{9,... | collective-permute-start | bytes 552968 | tf_op jit(solution)/shard_map/ppermute | solution.py:290
  15.3 34.6 %collective-permute-start.14 = (bf16[1,96,768]{2,1,0:T(8,128)(2,1)S(1)}, bf16[1,96,768]{2,1,0:T(8,128)(2,1)S(1)}, u32[]{:S(2)}, u32[]{:S(2)}) collective-permute-start(bf16[1,96,768]{2,1,0:T(8,128)(2,1)S(1)} %get-tuple-element.73), channel_id=1, source_target_pairs={{0,16},{1,17},{2,18},{3,19},{4,20},{5,21},{6,22},{7,23},{8,24},{9,... | collective-permute-start | bytes 442376 | tf_op jit(solution)/shard_map/ppermute | solution.py:290
  24.5 12.2 %collective-permute-start.5 = (bf16[2,96,768]{2,1,0:T(8,128)(2,1)S(1)}, bf16[2,96,768]{2,1,0:T(8,128)(2,1)S(1)}, u32[]{:S(2)}, u32[]{:S(2)}) collective-permute-start(bf16[2,96,768]{2,1,0:T(8,128)(2,1)S(1)} %pad_maximum_fusion.9), channel_id=1, source_target_pairs={{0,8},{1,9},{2,10},{3,11},{4,12},{5,13},{6,14},{7,15},{8,0},{9,1},... | collective-permute-start | bytes 884744 | tf_op jit(solution)/shard_map/ppermute | solution.py:290
  28.5 15.9 %collective-permute-start.10 = (bf16[2,240,384]{2,1,0:T(8,128)(2,1)S(1)}, bf16[2,240,384]{2,1,0:T(8,128)(2,1)S(1)}, u32[]{:S(2)}, u32[]{:S(2)}) collective-permute-start(bf16[2,240,384]{2,1,0:T(8,128)(2,1)S(1)} %pad_maximum_fusion.8), channel_id=1, source_target_pairs={{0,8},{1,9},{2,10},{3,11},{4,12},{5,13},{6,14},{7,15},{8,0},{9,1},... | collective-permute-start | bytes 1105928 | tf_op jit(solution)/shard_map/ppermute | solution.py:290
  36.8 14.2 %collective-permute-start.6 = (bf16[4,96,768]{2,1,0:T(8,128)(2,1)S(1)}, bf16[4,96,768]{2,1,0:T(8,128)(2,1)S(1)}, u32[]{:S(2)}, u32[]{:S(2)}) collective-permute-start(bf16[4,96,768]{2,1,0:T(8,128)(2,1)S(1)} %pad_maximum_fusion.6), channel_id=1, source_target_pairs={{0,4},{1,3},{2,6},{3,1},{4,0},{5,7},{6,2},{7,5},{8,12},{9,11},{10,... | collective-permute-start | bytes 1769480 | tf_op jit(solution)/shard_map/ppermute | solution.py:290
  44.5 16.4 %collective-permute-start.11 = (bf16[4,240,384]{2,1,0:T(8,128)(2,1)S(1)}, bf16[4,240,384]{2,1,0:T(8,128)(2,1)S(1)}, u32[]{:S(2)}, u32[]{:S(2)}) collective-permute-start(bf16[4,240,384]{2,1,0:T(8,128)(2,1)S(1)} %pad_maximum_fusion.5), channel_id=1, source_target_pairs={{0,4},{1,3},{2,6},{3,1},{4,0},{5,7},{6,2},{7,5},{8,12},{9,11},{10,... | collective-permute-start | bytes 2211848 | tf_op jit(solution)/shard_map/ppermute | solution.py:290
  52.1 26.4 %collective-permute-start.7 = (bf16[8,96,768]{2,1,0:T(8,128)(2,1)}, bf16[8,96,768]{2,1,0:T(8,128)(2,1)}, u32[]{:S(2)}, u32[]{:S(2)}) collective-permute-start(bf16[8,96,768]{2,1,0:T(8,128)(2,1)} %pad_maximum_fusion.1), channel_id=1, source_target_pairs={{0,2},{1,5},{2,0},{3,7},{4,6},{5,1},{6,4},{7,3},{8,10},{9,13},{10,... | collective-permute-start | bytes 3538952 | tf_op jit(solution)/shard_map/ppermute | solution.py:290
  59.3 16.6 %collective-permute-start.16 = (bf16[4,96,768]{2,1,0:T(8,128)(2,1)}, bf16[4,96,768]{2,1,0:T(8,128)(2,1)}, u32[]{:S(2)}, u32[]{:S(2)}) collective-permute-start(bf16[4,96,768]{2,1,0:T(8,128)(2,1)} %pad_maximum_fusion.7), channel_id=1, source_target_pairs={{0,4},{1,3},{2,6},{3,1},{4,0},{5,7},{6,2},{7,5},{8,12},{9,11},{10,... | collective-permute-start | bytes 1769480 | tf_op jit(solution)/shard_map/ppermute | solution.py:290
  62.1 28.6 %collective-permute-start.12 = (bf16[8,240,384]{2,1,0:T(8,128)(2,1)}, bf16[8,240,384]{2,1,0:T(8,128)(2,1)}, u32[]{:S(2)}, u32[]{:S(2)}) collective-permute-start(bf16[8,240,384]{2,1,0:T(8,128)(2,1)} %pad_maximum_fusion), channel_id=1, source_target_pairs={{0,2},{1,5},{2,0},{3,7},{4,6},{5,1},{6,4},{7,3},{8,10},{9,13},{10,... | collective-permute-start | bytes 4423688 | tf_op jit(solution)/shard_map/ppermute | solution.py:290
  77.1 26.2 %collective-permute-start.17 = (bf16[8,96,768]{2,1,0:T(8,128)(2,1)S(1)}, bf16[8,96,768]{2,1,0:T(8,128)(2,1)S(1)}, u32[]{:S(2)}, u32[]{:S(2)}) collective-permute-start(bf16[8,96,768]{2,1,0:T(8,128)(2,1)S(1)} %pad_maximum_fusion.2), channel_id=1, source_target_pairs={{0,2},{1,5},{2,0},{3,7},{4,6},{5,1},{6,4},{7,3},{8,10},{9,13},{10,... | collective-permute-start | bytes 3538952 | tf_op jit(solution)/shard_map/ppermute | solution.py:290
  80.9 33.0 %collective-permute-start.8 = (bf16[16,96,768]{2,1,0:T(8,128)(2,1)}, bf16[16,96,768]{2,1,0:T(8,128)(2,1)}, u32[]{:S(2)}, u32[]{:S(2)}) collective-permute-start(bf16[16,96,768]{2,1,0:T(8,128)(2,1)} %constant_dynamic-update-slice_fusion.5.mine.refs_5_), channel_id=1, source_target_pairs={{0,1},{1,0},{2,3},{3,2},{4,5},{5,4},{6,7},{7,6},{8,9},{9,8},{10,11... | collective-permute-start | bytes 7077896 | tf_op jit(solution)/shard_map/ppermute | solution.py:284
  93.5 52.6 %collective-permute-start.13 = (bf16[16,240,384]{2,1,0:T(8,128)(2,1)}, bf16[16,240,384]{2,1,0:T(8,128)(2,1)}, u32[]{:S(2)}, u32[]{:S(2)}) collective-permute-start(bf16[16,240,384]{2,1,0:T(8,128)(2,1)} %constant_dynamic-update-slice_fusion.15.refs_5_), channel_id=1, source_target_pairs={{0,1},{1,0},{2,3},{3,2},{4,5},{5,4},{6,7},{7,6},{8,9},{9,8},{10,11... | collective-permute-start | bytes 8847368 | tf_op jit(solution)/shard_map/ppermute | solution.py:284
  93.6 11.0 %collective-permute-start.1 = (bf16[2,12,48]{2,1,0:T(8,128)(2,1)S(1)}, bf16[2,12,48]{2,1,0:T(8,128)(2,1)S(1)}, u32[]{:S(2)}, u32[]{:S(2)}) collective-permute-start(bf16[2,12,48]{2,1,0:T(8,128)(2,1)S(1)} %pad_maximum_fusion.15), channel_id=1, source_target_pairs={{0,8},{1,9},{2,10},{3,11},{4,12},{5,13},{6,14},{7,15},{8,0},{9,1},... | collective-permute-start | bytes 6920 | tf_op jit(solution)/shard_map/ppermute | solution.py:290
  104.5 41.7 %collective-permute-start.18 = (bf16[16,96,768]{2,1,0:T(8,128)(2,1)}, bf16[16,96,768]{2,1,0:T(8,128)(2,1)}, u32[]{:S(2)}, u32[]{:S(2)}) collective-permute-start(bf16[16,96,768]{2,1,0:T(8,128)(2,1)} %constant_dynamic-update-slice_fusion.20.refs_7_), channel_id=1, source_target_pairs={{0,1},{1,0},{2,3},{3,2},{4,5},{5,4},{6,7},{7,6},{8,9},{9,8},{10,11... | collective-permute-start | bytes 7077896 | tf_op jit(solution)/shard_map/ppermute | solution.py:284
  232.4 18.9 %collective-permute-start.31 = (bf16[16,96,768]{2,1,0:T(8,128)(2,1)}, bf16[16,96,768]{2,1,0:T(8,128)(2,1)}, u32[]{:S(2)}, u32[]{:S(2)}) collective-permute-start(bf16[16,96,768]{2,1,0:T(8,128)(2,1)} %get-tuple-element.53), channel_id=1, source_target_pairs={{0,1},{1,0},{2,3},{3,2},{4,5},{5,4},{6,7},{7,6},{8,9},{9,8},{10,11... | collective-permute-start | bytes 7077896 | tf_op jit(solution)/shard_map/ppermute | solution.py:284
  232.9 61.5 %collective-permute-start.25 = (bf16[16,240,384]{2,1,0:T(8,128)(2,1)}, bf16[16,240,384]{2,1,0:T(8,128)(2,1)}, u32[]{:S(2)}, u32[]{:S(2)}) collective-permute-start(bf16[16,240,384]{2,1,0:T(8,128)(2,1)} %get-tuple-element.51), channel_id=1, source_target_pairs={{0,1},{1,0},{2,3},{3,2},{4,5},{5,4},{6,7},{7,6},{8,9},{9,8},{10,11... | collective-permute-start | bytes 8847368 | tf_op jit(solution)/shard_map/ppermute | solution.py:284
  243.2 38.2 %collective-permute-start.20 = (bf16[8,96,768]{2,1,0:T(8,128)(2,1)}, bf16[8,96,768]{2,1,0:T(8,128)(2,1)S(1)}, u32[]{:S(2)}, u32[]{:S(2)}) collective-permute-start(bf16[8,96,768]{2,1,0:T(8,128)(2,1)} %slice.287), channel_id=1, source_target_pairs={{0,2},{1,5},{2,0},{3,7},{4,6},{5,1},{6,4},{7,3},{8,10},{9,13},{10,... | collective-permute-start | bytes 3538952 | tf_op jit(solution)/shard_map/ppermute | solution.py:302
  254.5 29.2 %collective-permute-start.32 = (bf16[8,96,768]{2,1,0:T(8,128)(2,1)S(1)}, bf16[8,96,768]{2,1,0:T(8,128)(2,1)S(1)}, u32[]{:S(2)}, u32[]{:S(2)}) collective-permute-start(bf16[8,96,768]{2,1,0:T(8,128)(2,1)S(1)} %slice.317), channel_id=1, source_target_pairs={{0,2},{1,5},{2,0},{3,7},{4,6},{5,1},{6,4},{7,3},{8,10},{9,13},{10,... | collective-permute-start | bytes 3538952 | tf_op jit(solution)/shard_map/ppermute | solution.py:302
  255.4 17.5 %collective-permute-start.37 = (f32[8,12,48]{2,1,0:T(8,128)S(1)}, f32[8,12,48]{2,1,0:T(8,128)S(1)}, u32[]{:S(2)}, u32[]{:S(2)}) collective-permute-start(f32[8,12,48]{2,1,0:T(8,128)S(1)} %slice.325), channel_id=1, source_target_pairs={{0,2},{1,5},{2,0},{3,7},{4,6},{5,1},{6,4},{7,3},{8,10},{9,13},{10,... | collective-permute-start | bytes 55304 | tf_op jit(solution)/shard_map/ppermute | solution.py:302
  281.4 17.3 %collective-permute-start.40 = (f32[1,12,48]{2,1,0:T(8,128)}, f32[1,12,48]{2,1,0:T(8,128)}, u32[]{:S(2)}, u32[]{:S(2)}) collective-permute-start(f32[1,12,48]{2,1,0:T(8,128)} %slice.331), channel_id=1, source_target_pairs={{0,16},{1,17},{2,18},{3,19},{4,20},{5,21},{6,22},{7,23},{8,24},{9,... | collective-permute-start | bytes 6920 | tf_op jit(solution)/shard_map/ppermute | solution.py:302
  282.4 17.1 %collective-permute-start.21 = (bf16[4,96,768]{2,1,0:T(8,128)(2,1)}, bf16[4,96,768]{2,1,0:T(8,128)(2,1)S(1)}, u32[]{:S(2)}, u32[]{:S(2)}) collective-permute-start(bf16[4,96,768]{2,1,0:T(8,128)(2,1)} %slice.289), channel_id=1, source_target_pairs={{0,4},{1,3},{2,6},{3,1},{4,0},{5,7},{6,2},{7,5},{8,12},{9,11},{10,... | collective-permute-start | bytes 1769480 | tf_op jit(solution)/shard_map/ppermute | solution.py:302
  284.7 16.9 %collective-permute-start.33 = (bf16[4,96,768]{2,1,0:T(8,128)(2,1)}, bf16[4,96,768]{2,1,0:T(8,128)(2,1)}, u32[]{:S(2)}, u32[]{:S(2)}) collective-permute-start(bf16[4,96,768]{2,1,0:T(8,128)(2,1)} %slice.319), channel_id=1, source_target_pairs={{0,4},{1,3},{2,6},{3,1},{4,0},{5,7},{6,2},{7,5},{8,12},{9,11},{10,... | collective-permute-start | bytes 1769480 | tf_op jit(solution)/shard_map/ppermute | solution.py:302
  297.2 23.1 %collective-permute-start.26 = (bf16[8,240,384]{2,1,0:T(8,128)(2,1)S(1)}, bf16[8,240,384]{2,1,0:T(8,128)(2,1)S(1)}, u32[]{:S(2)}, u32[]{:S(2)}) collective-permute-start(bf16[8,240,384]{2,1,0:T(8,128)(2,1)S(1)} %slice.298), channel_id=1, source_target_pairs={{0,2},{1,5},{2,0},{3,7},{4,6},{5,1},{6,4},{7,3},{8,10},{9,13},{10,... | collective-permute-start | bytes 4423688 | tf_op jit(solution)/shard_map/ppermute | solution.py:302
  299.6 9.9 %collective-permute-start.22 = (bf16[2,96,768]{2,1,0:T(8,128)(2,1)S(1)}, bf16[2,96,768]{2,1,0:T(8,128)(2,1)S(1)}, u32[]{:S(2)}, u32[]{:S(2)}) collective-permute-start(bf16[2,96,768]{2,1,0:T(8,128)(2,1)S(1)} %slice.291), channel_id=1, source_target_pairs={{0,8},{1,9},{2,10},{3,11},{4,12},{5,13},{6,14},{7,15},{8,0},{9,1},... | collective-permute-start | bytes 884744 | tf_op jit(solution)/shard_map/ppermute | solution.py:302
  302.7 16.0 %collective-permute-start.34 = (bf16[2,96,768]{2,1,0:T(8,128)(2,1)S(1)}, bf16[2,96,768]{2,1,0:T(8,128)(2,1)S(1)}, u32[]{:S(2)}, u32[]{:S(2)}) collective-permute-start(bf16[2,96,768]{2,1,0:T(8,128)(2,1)S(1)} %slice.321), channel_id=1, source_target_pairs={{0,8},{1,9},{2,10},{3,11},{4,12},{5,13},{6,14},{7,15},{8,0},{9,1},... | collective-permute-start | bytes 884744 | tf_op jit(solution)/shard_map/ppermute | solution.py:302
  309.6 19.0 %collective-permute-start.23 = (bf16[1,96,768]{2,1,0:T(8,128)(2,1)S(1)}, bf16[1,96,768]{2,1,0:T(8,128)(2,1)S(1)}, u32[]{:S(2)}, u32[]{:S(2)}) collective-permute-start(bf16[1,96,768]{2,1,0:T(8,128)(2,1)S(1)} %slice.293), channel_id=1, source_target_pairs={{0,16},{1,17},{2,18},{3,19},{4,20},{5,21},{6,22},{7,23},{8,24},{9,... | collective-permute-start | bytes 442376 | tf_op jit(solution)/shard_map/ppermute | solution.py:302
  318.8 9.7 %collective-permute-start.35 = (bf16[1,96,768]{2,1,0:T(8,128)(2,1)S(1)}, bf16[1,96,768]{2,1,0:T(8,128)(2,1)S(1)}, u32[]{:S(2)}, u32[]{:S(2)}) collective-permute-start(bf16[1,96,768]{2,1,0:T(8,128)(2,1)S(1)} %slice.323), channel_id=1, source_target_pairs={{0,16},{1,17},{2,18},{3,19},{4,20},{5,21},{6,22},{7,23},{8,24},{9,... | collective-permute-start | bytes 442376 | tf_op jit(solution)/shard_map/ppermute | solution.py:302
  320.5 11.5 %collective-permute-start.27 = (bf16[4,240,384]{2,1,0:T(8,128)(2,1)S(1)}, bf16[4,240,384]{2,1,0:T(8,128)(2,1)S(1)}, u32[]{:S(2)}, u32[]{:S(2)}) collective-permute-start(bf16[4,240,384]{2,1,0:T(8,128)(2,1)S(1)} %slice.300), channel_id=1, source_target_pairs={{0,4},{1,3},{2,6},{3,1},{4,0},{5,7},{6,2},{7,5},{8,12},{9,11},{10,... | collective-permute-start | bytes 2211848 | tf_op jit(solution)/shard_map/ppermute | solution.py:302
  332.3 9.9 %collective-permute-start.28 = (bf16[2,240,384]{2,1,0:T(8,128)(2,1)S(1)}, bf16[2,240,384]{2,1,0:T(8,128)(2,1)S(1)}, u32[]{:S(2)}, u32[]{:S(2)}) collective-permute-start(bf16[2,240,384]{2,1,0:T(8,128)(2,1)S(1)} %slice.302), channel_id=1, source_target_pairs={{0,8},{1,9},{2,10},{3,11},{4,12},{5,13},{6,14},{7,15},{8,0},{9,1},... | collective-permute-start | bytes 1105928 | tf_op jit(solution)/shard_map/ppermute | solution.py:302
  342.2 9.4 %collective-permute-start.29 = (bf16[1,240,384]{2,1,0:T(8,128)(2,1)S(1)}, bf16[1,240,384]{2,1,0:T(8,128)(2,1)S(1)}, u32[]{:S(2)}, u32[]{:S(2)}) collective-permute-start(bf16[1,240,384]{2,1,0:T(8,128)(2,1)S(1)} %slice.304), channel_id=1, source_target_pairs={{0,16},{1,17},{2,18},{3,19},{4,20},{5,21},{6,22},{7,23},{8,24},{9,... | collective-permute-start | bytes 552968 | tf_op jit(solution)/shard_map/ppermute | solution.py:302
  (30 other events, 207.3 us)
